TPU v7x, 128 devices: a whole 4x4x4 slice. The times are simulated.
128 devices in a mesh: seq: 64 (over y, x_hi, z, core), head: 2 (over x_lo).
Axes of the slice: x: 4 (x_hi: 2, x_lo: 2; x = x_hi * 2 + x_lo), y: 4, z: 4, core: 2. Of those that a mesh axis runs over, the one named last changes fastest.
Arguments:
- features: bfloat16 [65536, 1024], P('seq', 'head'), may hold values from -4.1875 to 4.1875
- cells: int32 [65536], P('seq'), may hold values from 0 to 65535, as said below
- conv7: bfloat16 [7, 7, 1024], P(None, None, 'head'), may hold values from -0.875 to 0.875
- conv5: bfloat16 [5, 5, 1024], P(None, None, 'head'), may hold values from -1.25 to 1.25
- conv3: bfloat16 [3, 3, 1024], P(None, None, 'head'), may hold values from -2 to 2
- conv_bias: bfloat16 [1024], P('head'), may hold values from -3 to 3
- w_qkv: bfloat16 [1024, 3, 1024], P(None, None, 'head'), may hold values from -5 to 5
Outputs:
- attended: bfloat16 [65536, 1024], P('seq', 'head')
Inputs may be any that keep to these rules, and one draw needn't show every extreme that they name: cells names each of the 65536 grid cells once. Of the 1024 entries held by one index of seq, at most 32 lie in any one band of 1024 consecutive cells, and exactly 32 lie in some band; every band receives exactly 32 from some index of seq.
All inputs are finite; a program needn't handle non-finite values.
Results may differ from a plain program's by a relative error of at most 0.0052.
Values may be sent and summed in bfloat16 or wider, within the bound.
No kernel may reach another device: no remote copies, remote signals or barrier semaphores. Data moves between devices by JAX's collectives and lax.ppermute only.
A program may use at most 128 MiB of HBM per device.

v0:
```python
import math

import jax
import jax.numpy as jnp
from jax import lax
from jax.sharding import PartitionSpec as P

D = 1024
HEADS = 16
GRID_W = 256


def with_halo(shard, sides, width):
    for axis, dim in sides:
        count, length = (lax.axis_size(axis), shard.shape[dim])
        up = [(i, (i + 1) % count) for i in range(count - 1)]
        down = [(j, i) for i, j in up]
        last = lax.slice_in_dim(shard, length - width, length, axis=dim)
        first = lax.slice_in_dim(shard, 0, width, axis=dim)
        before = lax.ppermute(last, axis, up)
        after = lax.ppermute(first, axis, down)
        shard = jnp.concatenate([before, shard, after], axis=dim)
    return shard


def passed_along(block, axis, distance):
    devices = range(lax.axis_size(axis))
    route = [((i - distance) % len(devices), i) for i in devices]
    return lax.ppermute(block, axis, route)


def depthwise(padded, kernel, margin, height, width):
    reach = kernel.shape[0]
    result = jnp.zeros((height, width, padded.shape[2]), jnp.float32)
    for i in range(reach):
        for j in range(reach):
            result = result + padded[
                margin + i : margin + i + height, margin + j : margin + j + width
            ] * kernel[i, j].astype(jnp.float32)
    return result


def mix(extended, band_rows, width, conv7, conv5, conv3, conv_bias):
    padded = jnp.pad(extended, ((0, 0), (3, 3), (0, 0))).astype(jnp.float32)
    mixed_sum = padded[3 : 3 + band_rows, 3 : 3 + width] + conv_bias.astype(jnp.float32)
    for kernel in (conv7, conv5, conv3):
        mixed_sum = mixed_sum + depthwise(
            padded, kernel, 3 - kernel.shape[0] // 2, band_rows, width
        )
    return mixed_sum.astype(jnp.bfloat16).reshape(band_rows * width, extended.shape[2])


def attend_block(queries, own_keys, own_values, prior_keys, prior_values, score_scale):
    own_scores = (
        jnp.einsum("qhd,khd->qhk", queries, own_keys, preferred_element_type=jnp.float32)
        * score_scale
    )
    prior_scores = (
        jnp.einsum("qhd,khd->qhk", queries, prior_keys, preferred_element_type=jnp.float32)
        * score_scale
    )
    row_top = jnp.maximum(jnp.max(own_scores, axis=2), jnp.max(prior_scores, axis=2))[:, :, None]
    own_weight = jnp.exp(own_scores - row_top)
    prior_weight = jnp.exp(prior_scores - row_top)
    weight_sum = jnp.sum(own_weight, axis=2) + jnp.sum(prior_weight, axis=2)
    summed = jnp.einsum(
        "qhk,khd->qhd",
        own_weight.astype(jnp.bfloat16),
        own_values,
        preferred_element_type=jnp.float32,
    )
    summed = summed + jnp.einsum(
        "qhk,khd->qhd",
        prior_weight.astype(jnp.bfloat16),
        prior_values,
        preferred_element_type=jnp.float32,
    )
    return (summed / weight_sum[:, :, None]).astype(jnp.bfloat16)


def shards(features, cells, conv7, conv5, conv3, conv_bias, w_qkv):
    tok_dev, local_dim = features.shape
    members = lax.axis_size("seq")
    capacity = 2 * tok_dev // members
    owner_band = cells // tok_dev
    within = cells - owner_band * tok_dev
    onehot = (owner_band[:, None] == jnp.arange(members, dtype=jnp.int32)[None, :]).astype(
        jnp.int32
    )
    earlier = jnp.cumsum(onehot, axis=0) - onehot
    slot_index = owner_band * capacity + jnp.sum(earlier * onehot, axis=1)
    outgoing = jnp.zeros((members * capacity, local_dim), jnp.bfloat16).at[slot_index].set(features)
    targets = jnp.full((members * capacity,), tok_dev, jnp.int32).at[slot_index].set(within)
    arrived, places = (
        lax.all_to_all(outgoing, "seq", split_axis=0, concat_axis=0, tiled=True),
        lax.all_to_all(targets, "seq", split_axis=0, concat_axis=0, tiled=True),
    )
    band_grid = jnp.zeros((tok_dev + 1, local_dim), jnp.bfloat16).at[places].set(arrived)[:tok_dev]
    band_rows = tok_dev // GRID_W
    band_grid = band_grid.reshape(band_rows, GRID_W, local_dim)
    extended = with_halo(band_grid, (("seq", 0),), 3)
    ppeg = mix(extended, band_rows, GRID_W, conv7, conv5, conv3, conv_bias)
    weights = w_qkv.reshape(w_qkv.shape[0], 3 * local_dim)
    projected = jnp.dot(
        lax.all_gather(ppeg, "head", axis=1, tiled=True),
        weights,
        preferred_element_type=jnp.float32,
    ).astype(jnp.bfloat16)
    prior_keys, prior_values = passed_along(
        (projected[:, local_dim : 2 * local_dim], projected[:, 2 * local_dim :]), "seq", 1
    )
    head_dim = D // HEADS
    head_count = local_dim // head_dim
    score_scale = 1.0 / math.sqrt(head_dim)

    def to_heads(matrix):
        return matrix.reshape(tok_dev, head_count, head_dim)

    own_keys = to_heads(projected[:, local_dim : 2 * local_dim])
    own_values = to_heads(projected[:, 2 * local_dim :])
    prior_key_heads = to_heads(prior_keys)
    prior_value_heads = to_heads(prior_values)
    block_rows = min(512, tok_dev)
    query_blocks = projected[:, :local_dim].reshape(
        tok_dev // block_rows, block_rows, head_count, head_dim
    )
    attended = lax.map(
        lambda query_block: attend_block(
            query_block, own_keys, own_values, prior_key_heads, prior_value_heads, score_scale
        ),
        query_blocks,
    )
    return attended.reshape(tok_dev, local_dim)


def solution(mesh):
    placed = (
        P("seq", "head"),
        P("seq"),
        P(None, None, "head"),
        P(None, None, "head"),
        P(None, None, "head"),
        P("head"),
        P(None, None, "head"),
    )
    return jax.shard_map(
        shards, mesh=mesh, in_specs=placed, out_specs=P("seq", "head"), check_vma=False
    )
```

profile of v0, /device:TPU:8, one launch (start us, length us, event | category | flops | bytes accessed | tf_op | source)
XLA Modules:
  0.0 325.5 jit_solution(10241816885953619809)
XLA Ops:
  7.3 18.0 %reduce-window.6 = s32[64,8,128]{2,1,0:T(8,128)S(1)} reduce-window(s32[64,8,128]{2,1,0:T(8,128)S(1)} %fusion.100, s32[]{:T(128)} %copy.51), window={size=1x1x128 pad=0_0x0_0x127_0}, to_apply=%region_0.1 | reduce-window | flops 8323072 | bytes 524292 | tf_op jit(solution)/shard_map/reduce-window
  26.0 4.3 %scatter_custom_fusion = s32[2048]{0:T(1024)S(1)} fusion(s32[1024]{0:T(1024)S(1)} %get-tuple-element.173, s32[1024]{0:T(1024)S(1)} %get-tuple-element.172, s32[]{:T(128)} %constant.44.clone.1), kind=kCustom, calls=%fused_computation.137 | custom fusion | bytes 8196 | tf_op jit(solution)/shard_map/scatter | solution.py:93
  31.0 11.4 %all-to-all-start = ((s32[64,32,1]{1,2,0:T(1,128)}), s32[64,32,1]{1,2,0:T(1,128)S(1)}, u32[]{:S(2)}, u32[]{:S(2)}) async-start(s32[64,32,1]{1,2,0:T(1,128)} %bitcast.8), calls=%async_computation | async-start | bytes 65536 | tf_op jit(solution)/shard_map/all_to_all | solution.py:96
  42.4 7.2 %scatter_custom_fusion.1 = bf16[2048,512]{1,0:T(8,128)(2,1)} fusion(s32[1024]{0:T(1024)S(1)} %get-tuple-element.173, bf16[1024,512]{1,0:T(8,128)(2,1)} %param.9, bf16[]{:T(256)} %constant.30.clone.1), kind=kCustom, calls=%fused_computation.116 | custom fusion | bytes 2097664 | tf_op jit(solution)/shard_map/scatter | solution.py:92
  50.9 9.2 %all-to-all-start.1 = ((bf16[64,32,512]{2,1,0:T(8,128)(2,1)}), bf16[64,32,512]{2,1,0:T(8,128)(2,1)S(1)}, u32[]{:S(2)}, u32[]{:S(2)}) async-start(bf16[64,32,512]{2,1,0:T(8,128)(2,1)} %bitcast.10), calls=%async_computation.1 | async-start | bytes 4194304 | tf_op jit(solution)/shard_map/all_to_all | solution.py:95
  61.6 27.7 %all-to-all-done.1 = bf16[64,32,512]{2,1,0:T(8,128)(2,1)S(1)} async-done(((bf16[64,32,512]{2,1,0:T(8,128)(2,1)}), bf16[64,32,512]{2,1,0:T(8,128)(2,1)S(1)}, u32[]{:S(2)}, u32[]{:S(2)}) %all-to-all-start.1) | async-done | bytes 2097184 | tf_op jit(solution)/shard_map/all_to_all | solution.py:95
  89.3 9.7 %scatter_custom_fusion.2 = bf16[1025,512]{1,0:T(8,128)(2,1)S(1)} fusion(s32[2048]{0:T(1024)S(1)} %bitcast.297, bf16[2048,512]{1,0:T(8,128)(2,1)S(1)} %bitcast.208, bf16[]{:T(256)} %constant.30.clone.1), kind=kCustom, calls=%fused_computation.118 | custom fusion | bytes 1049602 | tf_op jit(solution)/shard_map/scatter | solution.py:98
  99.1 2.4 collective-permute-start
  101.5 7.9 %collective-permute-start.1 = (bf16[3,256,512]{2,1,0:T(8,128)(2,1)S(1)}, bf16[3,256,512]{2,1,0:T(8,128)(2,1)S(1)}, u32[]{:S(2)}, u32[]{:S(2)}) collective-permute-start(bf16[3,256,512]{2,1,0:T(8,128)(2,1)S(1)} %bitcast.211), channel_id=1, source_target_pairs={{2,0},{4,2},{6,4},{8,6},{10,8},{12,10},{14,12},{16,14},{18,16},{20... | collective-permute-start | bytes 2359304 | tf_op jit(solution)/shard_map/ppermute | solution.py:21
  109.6 7.3 %collective-permute-done = bf16[3,256,512]{2,1,0:T(8,128)(2,1)S(1)} collective-permute-done((bf16[3,256,512]{2,1,0:T(8,128)(2,1)S(1)}, bf16[3,256,512]{2,1,0:T(8,128)(2,1)S(1)}, u32[]{:S(2)}, u32[]{:S(2)}) %collective-permute-start) | collective-permute-done | bytes 786464 | tf_op jit(solution)/shard_map/ppermute | solution.py:20
  118.7 2.8 fusion.40
  121.5 52.8 %fusion.45 = bf16[4,256,512]{2,1,0:T(8,128)(2,1)} fusion(f32[10,262,512]{2,1,0:T(8,128)} %fusion.40, f32[512]{0:T(512)S(1)} %bitcast.221, f32[512]{0:T(512)S(1)} %bitcast.222, f32[512]{0:T(512)S(1)} %bitcast.215, f32[512]{0:T(512)S(1)} %bitcast.216, f32[512]{0:T(512)S(1)} %bitcast.217, f32[512]{0:T(512)S(1)} %bitcast.218, f32[512]{0:T(512)S(1)} %bitcast.219, ...), kind=kLoop, calls=%fused_computation.45 | loop fusion | flops 88080384 | bytes 103981056 | tf_op jit(solution)/shard_map/convert_element_type | solution.py:50
  174.3 3.1 copy.28
  177.4 33.7 %all-gather.2.cloned.1.call-done = bf16[1024,1024]{1,0:T(8,128)(2,1)} async-done(((bf16[1024,512]{1,0:T(8,128)(2,1)}), bf16[1024,1024]{1,0:T(8,128)(2,1)}) %all-gather.2.cloned.1.call-update) | async-done | bytes 2097168 | tf_op jit(solution)/shard_map/all_gather | solution.py:105
  211.1 6.0 %convolution_convert_fusion = bf16[1024,1536]{1,0:T(8,128)(2,1)S(1)} fusion(bf16[1024,1024]{1,0:T(8,128)(2,1)} %all-gather.2.cloned.1.call-done, bf16[1024,1536]{0,1:T(8,128)(2,1)} %bitcast.207), kind=kOutput, calls=%fused_computation.33 | convolution fusion | flops 3222798336 | bytes 8388608 | tf_op jit(solution)/shard_map/dot_general | solution.py:104
  220.5 2.3 copy.32
  224.9 2.5 copy.34
  227.4 9.8 %collective-permute-done.2 = bf16[1024,512]{1,0:T(8,128)(2,1)} collective-permute-done((bf16[1024,512]{1,0:T(8,128)(2,1)S(1)}, bf16[1024,512]{1,0:T(8,128)(2,1)}, u32[]{:S(2)}, u32[]{:S(2)}) %collective-permute-start.2) | collective-permute-done | bytes 1048608 | tf_op jit(solution)/shard_map/ppermute | solution.py:29
  238.6 9.7 %collective-permute-done.3 = bf16[1024,512]{1,0:T(8,128)(2,1)} collective-permute-done((bf16[1024,512]{1,0:T(8,128)(2,1)}, bf16[1024,512]{1,0:T(8,128)(2,1)}, u32[]{:S(2)}, u32[]{:S(2)}) %collective-permute-start.3) | collective-permute-done | bytes 1048608 | tf_op jit(solution)/shard_map/ppermute | solution.py:29
  248.4 2.3 copy.33
  250.6 63.3 %while.10 = (s32[]{:T(128)}, bf16[2,512,8,64]{1,3,2,0:T(8,128)(2,1)}, bf16[2,512,8,64]{1,3,2,0:T(8,128)(2,1)S(1)}, bf16[1024,8,64]{0,2,1:T(8,128)(2,1)S(1)}, bf1...) while((s32[]{:T(128)}, ...), condition=%wide.region_11.12_spmd, body=%wide.region_6.11_spmd.sunk | while | flops 2215370752 | bytes 117146264 | solution.py:127
  250.6 8.1 %bitcast_reduce_fusion.5 = (f32[512,8]{0,1:T(8,128)S(1)}, f32[8,512,1024]{2,1,0:T(8,128)}) fusion(bf16[1024,8,64]{0,2,1:T(8,128)(2,1)S(1)} %get-tuple-element.250, bf16[2,512,8,64]{1,3,2,0:T(8,128)(2,1)S(1)} %get-tuple-element.249, s32[]{:T(128)} %get-tuple-element.239), kind=kOutput, calls=%fused_computation.7.clone.1 | convolution fusion | flops 545255424 | bytes 18366468 | tf_op jit(solution)/shard_map/while/body/eval_jaxpr/qhd,khd->qhk/dot_general | solution.py:55
  258.8 2.5 bitcast_reduce_fusion.4
  261.2 9.2 %fusion.130 = (f32[512,8]{0,1:T(8,128)S(1)}, f32[512,8]{0,1:T(8,128)S(1)}) fusion(f32[8,512,1024]{2,1,0:T(8,128)S(1)} %get-tuple-element.225, f32[512,8]{0,1:T(8,128)S(1)} %max.8, f32[8,512,1024]{2,1,0:T(8,128)} %get-tuple-element.228), kind=kLoop, calls=%fused_computation.11.clone.1 | loop fusion | flops 25157632 | bytes 33603584 | tf_op jit(solution)/shard_map/while/body/eval_jaxpr/reduce_sum | solution.py:65
  270.5 3.7 %fusion.129 = f32[8,512,64]{1,2,0:T(8,128)S(1)} fusion(bf16[1024,8,64]{0,2,1:T(8,128)(2,1)S(1)} %copy-done, f32[8,512,1024]{2,1,0:T(8,128)S(1)} %get-tuple-element.225, f32[512,8]{0,1:T(8,128)S(1)} %max.8), kind=kOutput, calls=%fused_computation.13.clone.1 | convolution fusion | flops 549453824 | bytes 18890752 | tf_op jit(solution)/shard_map/while/body/eval_jaxpr/qhk,khd->qhd/dot_general | solution.py:72
  274.2 8.1 %fusion.131 = bf16[2,512,8,64]{1,3,2,0:T(8,128)(2,1)} fusion(bf16[2,512,8,64]{1,3,2,0:T(8,128)(2,1)} %get-tuple-element.240, s32[]{:T(128)} %get-tuple-element.239, f32[8,512,64]{1,2,0:T(8,128)S(1)} %fusion.129, bf16[1024,8,64]{0,2,1:T(8,128)(2,1)S(1)} %copy-done.2, f32[8,512,1024]{2,1,0:T(8,128)} %get-tuple-element.228, f32[512,8]{0,1:T(8,128)S(1)} %max.8, ...), kind=kOutput, calls=%fused_computation.19.clone.1 | convolution fusion | flops 550240256 | bytes 19431936 | tf_op jit(solution)/shard_map/while/body/eval_jaxpr/qhk,khd->qhd/dot_general | solution.py:66
  282.3 8.1 %bitcast_reduce_fusion.5 = (f32[512,8]{0,1:T(8,128)S(1)}, f32[8,512,1024]{2,1,0:T(8,128)}) fusion(bf16[1024,8,64]{0,2,1:T(8,128)(2,1)S(1)} %get-tuple-element.250, bf16[2,512,8,64]{1,3,2,0:T(8,128)(2,1)S(1)} %get-tuple-element.249, s32[]{:T(128)} %get-tuple-element.239), kind=kOutput, calls=%fused_computation.7.clone.1 | convolution fusion | flops 545255424 | bytes 18366468 | tf_op jit(solution)/shard_map/while/body/eval_jaxpr/qhd,khd->qhk/dot_general | solution.py:55
  290.4 2.5 bitcast_reduce_fusion.4
  292.9 9.2 %fusion.130 = (f32[512,8]{0,1:T(8,128)S(1)}, f32[512,8]{0,1:T(8,128)S(1)}) fusion(f32[8,512,1024]{2,1,0:T(8,128)S(1)} %get-tuple-element.225, f32[512,8]{0,1:T(8,128)S(1)} %max.8, f32[8,512,1024]{2,1,0:T(8,128)} %get-tuple-element.228), kind=kLoop, calls=%fused_computation.11.clone.1 | loop fusion | flops 25157632 | bytes 33603584 | tf_op jit(solution)/shard_map/while/body/eval_jaxpr/reduce_sum | solution.py:65
  302.1 3.7 %fusion.129 = f32[8,512,64]{1,2,0:T(8,128)S(1)} fusion(bf16[1024,8,64]{0,2,1:T(8,128)(2,1)S(1)} %copy-done, f32[8,512,1024]{2,1,0:T(8,128)S(1)} %get-tuple-element.225, f32[512,8]{0,1:T(8,128)S(1)} %max.8), kind=kOutput, calls=%fused_computation.13.clone.1 | convolution fusion | flops 549453824 | bytes 18890752 | tf_op jit(solution)/shard_map/while/body/eval_jaxpr/qhk,khd->qhd/dot_general | solution.py:72
  305.8 8.1 %fusion.131 = bf16[2,512,8,64]{1,3,2,0:T(8,128)(2,1)} fusion(bf16[2,512,8,64]{1,3,2,0:T(8,128)(2,1)} %get-tuple-element.240, s32[]{:T(128)} %get-tuple-element.239, f32[8,512,64]{1,2,0:T(8,128)S(1)} %fusion.129, bf16[1024,8,64]{0,2,1:T(8,128)(2,1)S(1)} %copy-done.2, f32[8,512,1024]{2,1,0:T(8,128)} %get-tuple-element.228, f32[512,8]{0,1:T(8,128)S(1)} %max.8, ...), kind=kOutput, calls=%fused_computation.19.clone.1 | convolution fusion | flops 550240256 | bytes 19431936 | tf_op jit(solution)/shard_map/while/body/eval_jaxpr/qhk,khd->qhd/dot_general | solution.py:66
  313.9 2.6 copy.39
  (60 shorter events, 16.0 us)
Async XLA Ops:
  6.5 19.4 %copy-start.6 = (s32[1024]{0:T(1024)S(1)}, s32[1024]{0:T(1024)}, u32[]{:S(2)}) copy-start(s32[1024]{0:T(1024)} %param.10) | copy-start | bytes 12292
  31.0 19.9 %all-to-all-start = ((s32[64,32,1]{1,2,0:T(1,128)}), s32[64,32,1]{1,2,0:T(1,128)S(1)}, u32[]{:S(2)}, u32[]{:S(2)}) async-start(s32[64,32,1]{1,2,0:T(1,128)} %bitcast.8), calls=%async_computation | async-start | bytes 65536 | tf_op jit(solution)/shard_map/all_to_all | solution.py:96
  50.9 9.2 %copy-start.5 = (bf16[3,3,512]{2,1,0:T(4,128)(2,1)S(1)}, bf16[3,3,512]{2,1,0:T(4,128)(2,1)}, u32[]{:S(2)}) copy-start(bf16[3,3,512]{2,1,0:T(4,128)(2,1)} %param.13) | copy-start | bytes 27652
  50.9 9.3 %copy-start.3 = (bf16[7,7,512]{2,1,0:T(8,128)(2,1)S(1)}, bf16[7,7,512]{2,1,0:T(8,128)(2,1)}, u32[]{:S(2)}) copy-start(bf16[7,7,512]{2,1,0:T(8,128)(2,1)} %param.11) | copy-start | bytes 150532
  50.9 38.3 %all-to-all-start.1 = ((bf16[64,32,512]{2,1,0:T(8,128)(2,1)}), bf16[64,32,512]{2,1,0:T(8,128)(2,1)S(1)}, u32[]{:S(2)}, u32[]{:S(2)}) async-start(bf16[64,32,512]{2,1,0:T(8,128)(2,1)} %bitcast.10), calls=%async_computation.1 | async-start | bytes 4194304 | tf_op jit(solution)/shard_map/all_to_all | solution.py:95
  60.1 151.0 %all-gather.2.cloned.1.call-start = ((), (), s32[]{:S(2)}) async-start(), calls=%async_computation.2 | async-start | bytes 3145728 | tf_op jit(solution)/shard_map/all_gather | solution.py:105
  89.3 20.1 %copy-start.4 = (bf16[5,5,512]{2,1,0:T(8,128)(2,1)S(1)}, bf16[5,5,512]{2,1,0:T(8,128)(2,1)}, u32[]{:S(2)}) copy-start(bf16[5,5,512]{2,1,0:T(8,128)(2,1)} %param.12) | copy-start | bytes 76804
  89.3 20.2 %copy-start.7 = (bf16[512]{0:T(512)(128)(2,1)S(1)}, bf16[512]{0:T(512)(128)(2,1)}, u32[]{:S(2)}) copy-start(bf16[512]{0:T(512)(128)(2,1)} %param.14) | copy-start | bytes 3076
  99.1 17.8 %collective-permute-start = (bf16[3,256,512]{2,1,0:T(8,128)(2,1)S(1)}, bf16[3,256,512]{2,1,0:T(8,128)(2,1)S(1)}, u32[]{:S(2)}, u32[]{:S(2)}) collective-permute-start(bf16[3,256,512]{2,1,0:T(8,128)(2,1)S(1)} %bitcast.212), channel_id=1, source_target_pairs={{0,2},{2,4},{4,6},{6,8},{8,10},{10,12},{12,14},{14,16},{16,18},{18... | collective-permute-start | bytes 2359304 | tf_op jit(solution)/shard_map/ppermute | solution.py:20
  101.5 17.2 %collective-permute-start.1 = (bf16[3,256,512]{2,1,0:T(8,128)(2,1)S(1)}, bf16[3,256,512]{2,1,0:T(8,128)(2,1)S(1)}, u32[]{:S(2)}, u32[]{:S(2)}) collective-permute-start(bf16[3,256,512]{2,1,0:T(8,128)(2,1)S(1)} %bitcast.211), channel_id=1, source_target_pairs={{2,0},{4,2},{6,4},{8,6},{10,8},{12,10},{14,12},{16,14},{18,16},{20... | collective-permute-start | bytes 2359304 | tf_op jit(solution)/shard_map/ppermute | solution.py:21
  121.5 52.8 %copy-start.1 = (bf16[1024,3,512]{2,0,1:T(8,128)(2,1)S(1)}, bf16[1024,3,512]{2,0,1:T(8,128)(2,1)}, u32[]{:S(2)}) copy-start(bf16[1024,3,512]{2,0,1:T(8,128)(2,1)} %param.15) | copy-start | bytes 9437188
  218.3 18.8 %collective-permute-start.2 = (bf16[1024,512]{1,0:T(8,128)(2,1)S(1)}, bf16[1024,512]{1,0:T(8,128)(2,1)}, u32[]{:S(2)}, u32[]{:S(2)}) collective-permute-start(bf16[1024,512]{1,0:T(8,128)(2,1)S(1)} %get-tuple-element.85), channel_id=1, source_target_pairs={{126,0},{0,2},{2,4},{4,6},{6,8},{8,10},{10,12},{12,14},{14,16},{16... | collective-permute-start | bytes 3145736 | tf_op jit(solution)/shard_map/ppermute | solution.py:29
  218.3 30.1 %collective-permute-start.3 = (bf16[1024,512]{1,0:T(8,128)(2,1)}, bf16[1024,512]{1,0:T(8,128)(2,1)}, u32[]{:S(2)}, u32[]{:S(2)}) collective-permute-start(bf16[1024,512]{1,0:T(8,128)(2,1)} %get-tuple-element.84), channel_id=1, source_target_pairs={{126,0},{0,2},{2,4},{4,6},{6,8},{8,10},{10,12},{12,14},{14,16},{16... | collective-permute-start | bytes 3145736 | tf_op jit(solution)/shard_map/ppermute | solution.py:29
  261.2 9.2 %copy-start = (bf16[1024,8,64]{0,2,1:T(8,128)(2,1)S(1)}, bf16[1024,8,64]{0,2,1:T(8,128)(2,1)}, u32[]{:S(2)}) copy-start(bf16[1024,8,64]{0,2,1:T(8,128)(2,1)} %get-tuple-element.253) | copy-start | bytes 3145732 | tf_op jit(solution)/shard_map/while
  270.5 3.7 %copy-start.2 = (bf16[1024,8,64]{0,2,1:T(8,128)(2,1)S(1)}, bf16[1024,8,64]{0,2,1:T(8,128)(2,1)}, u32[]{:S(2)}) copy-start(bf16[1024,8,64]{0,2,1:T(8,128)(2,1)} %get-tuple-element.252) | copy-start | bytes 3145732 | tf_op jit(solution)/shard_map/while
  292.9 9.2 %copy-start = (bf16[1024,8,64]{0,2,1:T(8,128)(2,1)S(1)}, bf16[1024,8,64]{0,2,1:T(8,128)(2,1)}, u32[]{:S(2)}) copy-start(bf16[1024,8,64]{0,2,1:T(8,128)(2,1)} %get-tuple-element.253) | copy-start | bytes 3145732 | tf_op jit(solution)/shard_map/while
  302.1 3.7 %copy-start.2 = (bf16[1024,8,64]{0,2,1:T(8,128)(2,1)S(1)}, bf16[1024,8,64]{0,2,1:T(8,128)(2,1)}, u32[]{:S(2)}) copy-start(bf16[1024,8,64]{0,2,1:T(8,128)(2,1)} %get-tuple-element.252) | copy-start | bytes 3145732 | tf_op jit(solution)/shard_map/while
Sparse Core Ops, SparseCore 0:
  174.4 36.6 all-gather.1
where the time goes:
time: 328 us; the launch traced here: 325 us
  other arithmetic  93.9 us (29%)
  waiting for transfers between devices  91.3 us (28%)
  matrix products  50.7 us (15%)
  local copies, waits for them, and re-layouts  43.2 us (13%)
  starting transfers between devices  32.5 us (10%)
  between operations  13.7 us (4%)
    convert_element_type x1, other arithmetic, mix(): mixed_sum.astype(jnp.bfloat16).reshape(band_rows * width, extended.shape[2])  52.8 us
    all_gather x1, waiting for transfers between devices, shards(): lax.all_gather(ppeg, 'head', axis=1, tiled=True)  33.7 us
    all_to_all x1, waiting for transfers between devices, shards(): lax.all_to_all(outgoing, 'seq', split_axis=0, concat_axis=0, tiled=True)  27.7 us
    ppermute x2, waiting for transfers between devices, passed_along(): return lax.ppermute(block, axis, route)  19.5 us
    reduce_sum x2, other arithmetic, attend_block(): weight_sum = jnp.sum(own_weight, axis=2) + jnp.sum(prior_weight, axis=2)  18.4 us
    another operation x3, other arithmetic  18.2 us
    dot_general x2, matrix products, attend_block(): jnp.einsum('qhk,khd->qhd', own_weight.astype(jnp.bfloat16), own_values, p...  16.3 us
    dot_general x2, matrix products, attend_block(): jnp.einsum('qhd,khd->qhk', queries, own_keys, preferred_element_type=jnp....  16.2 us
  transfers between devices with their start and end apart: 7, of which 7 were waited for; matrix products, arithmetic and copies ran while one was open for 6% of the time, Pallas kernels for 0%

commit v1 on v0

v1 whole, which is shorter than its diff:
```python
import functools
import math

import jax
import jax.numpy as jnp
from jax import lax
from jax.experimental import pallas as pl
from jax.experimental.pallas import tpu as pltpu
from jax.sharding import PartitionSpec as P

D = 1024
HEADS = 16
GRID_W = 256
BANDS = 64
TOK = 1024
LOCAL = 512
CAP = 32
MSG = 4 * CAP + 8
BF16 = jnp.bfloat16
F32 = jnp.float32
VMEM_BYTES = 56 * 1024 * 1024


def iota(shape, dim):
    return lax.broadcasted_iota(jnp.int32, shape, dim)


def ones_where(mask):
    return jnp.where(mask, 1.0, 0.0).astype(BF16)


def params(**kwargs):
    return pltpu.CompilerParams(vmem_limit_bytes=VMEM_BYTES, **kwargs)


def pack_kernel(cells_ref, feat_ref, out_ref, slot_ref, info_ref):
    step = pl.program_id(0)

    @pl.when(step == 0)
    def _():
        cells = cells_ref[...]
        band = cells >> 10
        within = cells & (TOK - 1)
        member = jnp.where(iota((BANDS, TOK), 0) == band, 1.0, 0.0)
        before = ones_where(iota((TOK, TOK), 0) < iota((TOK, TOK), 1))
        counts = jnp.dot(member.astype(BF16), before, preferred_element_type=F32)
        rank = jnp.sum(member * counts, axis=0, keepdims=True).astype(jnp.int32)
        slot_ref[...] = band * CAP + rank
        place = (within & 768) | ((within & 31) << 3) | ((within >> 5) & 7)
        row = iota((16, TOK), 0)
        info = jnp.where(row == 0, (place >> 5) + 1, jnp.where(row == 1, place & 31, 0))
        info_ref[...] = info.astype(F32).astype(BF16)

    chosen = ones_where(slot_ref[...] - step * 256 == iota((256, TOK), 0))
    rows = jnp.dot(chosen, feat_ref[...], preferred_element_type=F32).astype(BF16)
    for c in range(4):
        out_ref[:, c * CAP : (c + 1) * CAP, :] = rows[:, c * 128 : (c + 1) * 128].reshape(8, CAP, 128)
    info = lax.dot_general(
        info_ref[...], chosen, (((1,), (1,)), ((), ())), preferred_element_type=F32
    )
    group = iota((8, 128), 1) // CAP
    for d in range(8):
        own = jnp.where(group == d % 4, info[:8, d // 4 * 128 : d // 4 * 128 + 128], 0.0)
        own = own + pltpu.roll(own, 64, 1)
        own = own + pltpu.roll(own, 32, 1)
        out_ref[d, 4 * CAP :, :] = own.astype(BF16)


def pack(cells, features):
    return pl.pallas_call(
        pack_kernel,
        grid=(8,),
        in_specs=[
            pl.BlockSpec((1, TOK), lambda i: (0, 0)),
            pl.BlockSpec((TOK, LOCAL), lambda i: (0, 0)),
        ],
        out_specs=pl.BlockSpec((8, MSG, 128), lambda i: (i, 0, 0)),
        out_shape=jax.ShapeDtypeStruct((BANDS, MSG, 128), BF16),
        scratch_shapes=[pltpu.VMEM((1, TOK), jnp.int32), pltpu.VMEM((16, TOK), BF16)],
        compiler_params=params(),
        name="pack",
    )(cells.reshape(1, TOK), features)


def place_kernel(msg_ref, out_ref, place_ref):
    step = pl.program_id(0)

    @pl.when(step == 0)
    def _():
        info = msg_ref[:, 4 * CAP :, :].astype(F32).reshape(16, 4, 8, 128)
        shape = (16, 4, 8, 128)
        info = jnp.sum(jnp.where(iota(shape, 3) // CAP == iota(shape, 1), info, 0.0), axis=1)
        place_ref[...] = (info[:, 0, :] * 32.0 + info[:, 1, :]).astype(jnp.int32) - 32

    cell = iota((256, 128), 0) + step * 256
    chosen = jnp.concatenate(
        [ones_where(place_ref[g : g + 1, :] == cell) for g in range(16)], axis=1
    )
    rows = jnp.concatenate(
        [msg_ref[:, c * CAP : (c + 1) * CAP, :].reshape(BANDS * CAP, 128) for c in range(4)],
        axis=1,
    )
    out_ref[...] = jnp.dot(chosen, rows, preferred_element_type=F32).astype(BF16)


def place(messages):
    return pl.pallas_call(
        place_kernel,
        grid=(4,),
        in_specs=[pl.BlockSpec((BANDS, MSG, 128), lambda i: (0, 0, 0))],
        out_specs=pl.BlockSpec((256, LOCAL), lambda i: (i, 0)),
        out_shape=jax.ShapeDtypeStruct((TOK, LOCAL), BF16),
        scratch_shapes=[pltpu.VMEM((16, 128), jnp.int32)],
        compiler_params=params(),
        name="place",
    )(messages)


def conv_kernel(band_ref, above_ref, below_ref, w_ref, bias_ref, out_ref, x_ref, tap_ref, nat_ref):
    sub = iota((3, 8, 128), 1)
    for r in range(10):
        if r < 3:
            rows = above_ref[r * 256 : (r + 1) * 256, :]
        elif r < 7:
            rows = band_ref[(r - 3) * 256 : (r - 2) * 256, :]
        else:
            rows = below_ref[(r - 7) * 256 : (r - 6) * 256, :]
        x = rows.astype(F32).reshape(32, 8, 128)
        x_ref[r, 3:35] = x
        x_ref[r, 0:3] = jnp.where(sub == 0, 0.0, pltpu.roll(x[29:32], 1, 1))
        x_ref[r, 35:38] = jnp.where(sub == 7, 0.0, pltpu.roll(x[0:3], 7, 1))
    for t in range(49):
        tap_ref[t] = jnp.broadcast_to(w_ref[t : t + 1, :], (8, 128))
    bias = jnp.broadcast_to(bias_ref[...], (8, 128))

    def group(g, carry):
        k = g * 4
        acc = [[bias] * 4 for _ in range(4)]
        for j in range(7):
            taps = [tap_ref[i * 7 + j] for i in range(7)]
            for r in range(10):
                for n in range(4):
                    x = x_ref[r, k + j + n]
                    for i in range(7):
                        if 0 <= r - i < 4:
                            acc[r - i][n] = acc[r - i][n] + x * taps[i]
        for o in range(4):
            for n in range(4):
                nat_ref[pl.ds(o * 256 + k + n, 8, stride=32), :] = acc[o][n]
        return carry

    lax.fori_loop(0, 8, group, 0)
    out_ref[...] = nat_ref[...].astype(BF16)


def conv(band, above, below, taps, bias):
    return pl.pallas_call(
        conv_kernel,
        grid=(4,),
        in_specs=[
            pl.BlockSpec((TOK, 128), lambda i: (0, i)),
            pl.BlockSpec((768, 128), lambda i: (0, i)),
            pl.BlockSpec((768, 128), lambda i: (0, i)),
            pl.BlockSpec((49, 128), lambda i: (0, i)),
            pl.BlockSpec((1, 128), lambda i: (0, i)),
        ],
        out_specs=pl.BlockSpec((TOK, 128), lambda i: (0, i)),
        out_shape=jax.ShapeDtypeStruct((TOK, LOCAL), BF16),
        scratch_shapes=[
            pltpu.VMEM((10, 38, 8, 128), F32),
            pltpu.VMEM((49, 8, 128), F32),
            pltpu.VMEM((TOK, 128), F32),
        ],
        compiler_params=params(),
        name="conv",
    )(band, above, below, taps, bias)


def project_kernel(half_ref, own_ref, other_ref, w_own_ref, w_other_ref, out_ref):
    out_ref[...] = (
        jnp.dot(own_ref[...], w_own_ref[...], preferred_element_type=F32)
        + jnp.dot(other_ref[...], w_other_ref[...], preferred_element_type=F32)
    ).astype(BF16)


def project(half, own, other, weights, first, width):
    rows = own.shape[0]
    return pl.pallas_call(
        project_kernel,
        grid_spec=pltpu.PrefetchScalarGridSpec(
            num_scalar_prefetch=1,
            grid=(rows // 256, width),
            in_specs=[
                pl.BlockSpec((256, LOCAL), lambda i, j, h: (i, 0)),
                pl.BlockSpec((256, LOCAL), lambda i, j, h: (i, 0)),
                pl.BlockSpec((LOCAL, LOCAL), lambda i, j, h: (h[0], first + j)),
                pl.BlockSpec((LOCAL, LOCAL), lambda i, j, h: (1 - h[0], first + j)),
            ],
            out_specs=pl.BlockSpec((256, LOCAL), lambda i, j, h: (i, j)),
        ),
        out_shape=jax.ShapeDtypeStruct((rows, width * LOCAL), BF16),
        compiler_params=params(),
        cost_estimate=pl.CostEstimate(
            flops=2 * rows * D * width * LOCAL,
            bytes_accessed=2 * (rows * D + (rows + D) * width * LOCAL),
            transcendentals=0,
        ),
        name="project",
    )(half, own, other, weights, weights)


def partial_attention(q_ref, k_ref, v_ref):
    q, k = q_ref[...], k_ref[...]
    lane = iota(q.shape, 1)
    v = jnp.concatenate([v_ref[...], jnp.ones(v_ref.shape, BF16)], axis=1)
    parts = []
    for head in range(2):
        mine = (lane // 64) == head
        scores = lax.dot_general(
            jnp.where(mine, q * 0.125, 0.0).astype(BF16),
            k,
            (((1,), (1,)), ((), ())),
            preferred_element_type=F32,
        )
        top = jnp.max(scores, axis=1, keepdims=True)
        weight = jnp.exp(scores - top).astype(BF16)
        summed = jnp.dot(weight, v, preferred_element_type=F32)
        parts.append((summed[:, :128], summed[:, 128:], jnp.broadcast_to(top, q.shape)))
    first = lane < 64
    return [jnp.where(first, a, b) for a, b in zip(*parts)]


def own_kernel(q_ref, k_ref, v_ref, acc_ref, sum_ref, top_ref):
    acc_ref[...], sum_ref[...], top_ref[...] = partial_attention(q_ref, k_ref, v_ref)


def prior_kernel(q_ref, k_ref, v_ref, acc_ref, sum_ref, top_ref, out_ref):
    acc, total, top = partial_attention(q_ref, k_ref, v_ref)
    highest = jnp.maximum(top, top_ref[...])
    here, there = jnp.exp(top - highest), jnp.exp(top_ref[...] - highest)
    total = total * here + sum_ref[...] * there
    out_ref[...] = ((acc * here + acc_ref[...] * there) / total).astype(BF16)


QROWS = 256


def attend(queries, keys_values, state=None):
    block = pl.BlockSpec((QROWS, 128), lambda p, i: (i, p))
    in_specs = [
        block,
        pl.BlockSpec((TOK, 128), lambda p, i: (0, p)),
        pl.BlockSpec((TOK, 128), lambda p, i: (0, 4 + p)),
    ]
    cost = pl.CostEstimate(
        flops=4 * TOK * TOK * LOCAL, bytes_accessed=10 * 2**20, transcendentals=8 * TOK * TOK
    )
    if state is None:
        return pl.pallas_call(
            own_kernel,
            grid=(4, TOK // QROWS),
            in_specs=in_specs,
            out_specs=[block] * 3,
            out_shape=[jax.ShapeDtypeStruct((TOK, LOCAL), F32)] * 3,
            compiler_params=params(),
            cost_estimate=cost,
            name="own_keys",
        )(queries, keys_values, keys_values)
    return pl.pallas_call(
        prior_kernel,
        grid=(4, TOK // QROWS),
        in_specs=in_specs + [block] * 3,
        out_specs=block,
        out_shape=jax.ShapeDtypeStruct((TOK, LOCAL), BF16),
        compiler_params=params(),
        cost_estimate=cost,
        name="prior_keys",
    )(queries, keys_values, keys_values, *state)


def merged_taps(conv7, conv5, conv3):
    taps = conv7.astype(F32)
    taps = taps + jnp.pad(conv5.astype(F32), ((1, 1), (1, 1), (0, 0)))
    taps = taps + jnp.pad(conv3.astype(F32), ((2, 2), (2, 2), (0, 0)))
    return taps.reshape(49, LOCAL) + (jnp.arange(49) == 24).astype(F32)[:, None]


def shards(features, cells, conv7, conv5, conv3, conv_bias, w_qkv):
    messages = pack(cells, features)
    arrived = lax.all_to_all(messages, "seq", split_axis=0, concat_axis=0, tiled=True)
    band = place(arrived)
    up = [(i, i + 1) for i in range(BANDS - 1)]
    down = [(j, i) for i, j in up]
    above = lax.ppermute(band[256:], "seq", up)
    below = lax.ppermute(band[:768], "seq", down)
    taps = merged_taps(conv7, conv5, conv3)
    ppeg = conv(band, above, below, taps, conv_bias.astype(F32).reshape(1, LOCAL))
    other = lax.ppermute(ppeg, "head", [(0, 1), (1, 0)])
    weights = w_qkv.reshape(D, 3 * LOCAL)
    half = lax.axis_index("head").astype(jnp.int32).reshape(1)
    keys_values = project(half, ppeg, other, weights, 1, 2)
    prior = lax.ppermute(keys_values, "seq", [(i, (i + 1) % BANDS) for i in range(BANDS)])
    queries = project(half, ppeg, other, weights, 0, 1)
    state = attend(queries, keys_values)
    return attend(queries, prior, state)


def solution(mesh):
    placed = (
        P("seq", "head"),
        P("seq"),
        P(None, None, "head"),
        P(None, None, "head"),
        P(None, None, "head"),
        P("head"),
        P(None, None, "head"),
    )
    return jax.shard_map(
        shards, mesh=mesh, in_specs=placed, out_specs=P("seq", "head"), check_vma=False
    )
```

time: 328 us -> 172 us (0.52)
  other arithmetic: 93.9 us -> 1.36 us
  Pallas kernels: 0 us -> 79.4 us
  waiting for transfers between devices: 91.3 us -> 31.4 us
  matrix products: 50.7 us -> 0 us
  blocking collectives: 0 us -> 43 us
  local copies, waits for them, and re-layouts: 43.2 us -> 9.88 us
  starting transfers between devices: 32.5 us -> 6.06 us
  between operations: 13.7 us -> 0.08 us
    pallas_call x0 -> x7, Pallas kernels: none -> 79.4 us  [the longest x1 20.7 us: attend(): pl.pallas_call(prior_kernel, grid=(4, TOK // QROWS), in_specs=in_specs +...]
    convert_element_type x4 -> x1, other arithmetic: 55.6 us -> 0.01 us  [merged_taps(): return taps.reshape(49, LOCAL) + (jnp.arange(49) == 24).astype(F32)[:, None]]
    dot_general x9 -> x0, matrix products: 50.7 us -> none  [the longest x2 16.3 us: attend_block(): jnp.einsum('qhk,khd->qhd', own_weight.astype(jnp.bfloat16), own_values, p...]
    all_to_all x0 -> x1, blocking collectives: none -> 43 us  [shards(): lax.all_to_all(messages, 'seq', split_axis=0, concat_axis=0, tiled=True)]
    all_gather x1 -> x0, waiting for transfers between devices: 33.7 us -> none  [shards(): lax.all_gather(ppeg, 'head', axis=1, tiled=True)]
    all_to_all x2 -> x0, waiting for transfers between devices: 29 us -> none  [the longest x1 27.7 us: shards(): lax.all_to_all(outgoing, 'seq', split_axis=0, concat_axis=0, tiled=True)]
    scatter x3 -> x0, local copies, waits for them, and re-layouts: 21.2 us -> none  [the longest x1 9.72 us: shards(): jnp.zeros((tok_dev + 1, local_dim), jnp.bfloat16).at[places].set(arrived)]
    all_to_all x2 -> x0, starting transfers between devices: 20.6 us -> none  [the longest x1 11.4 us: shards(): lax.all_to_all(targets, 'seq', split_axis=0, concat_axis=0, tiled=True)]
  transfers between devices with their start and end apart: 7 -> 4, of which waited for: 7 -> 4; matrix products, arithmetic and copies ran while one was open for 6% -> 4% of each run, Pallas kernels for 0% -> 15%
where the time goes in v1:
time: 172 us; the launch traced here: 171 us
  Pallas kernels  79.4 us (46%)
  blocking collectives  43 us (25%)
  waiting for transfers between devices  31.4 us (18%)
  local copies, waits for them, and re-layouts  9.88 us (6%)
  starting transfers between devices  6.06 us (4%)
    all_to_all x1, blocking collectives, shards(): lax.all_to_all(messages, 'seq', split_axis=0, concat_axis=0, tiled=True)  43 us
    pallas_call x1, Pallas kernels, attend(): pl.pallas_call(prior_kernel, grid=(4, TOK // QROWS), in_specs=in_specs +...  20.7 us
    pallas_call x1, Pallas kernels, attend(): pl.pallas_call(own_kernel, grid=(4, TOK // QROWS), in_specs=in_specs, out...  20.3 us
    pallas_call x2, Pallas kernels, project(): pl.pallas_call(project_kernel, grid_spec=pltpu.PrefetchScalarGridSpec(num...  13.8 us
    ppermute x1, waiting for transfers between devices, shards(): other = lax.ppermute(ppeg, 'head', [(0, 1), (1, 0)])  11.9 us
    pallas_call x1, Pallas kernels, conv(): pl.pallas_call(conv_kernel, grid=(4,), in_specs=[pl.BlockSpec((TOK, 128),...  11.5 us
    ppermute x1, waiting for transfers between devices, shards(): above = lax.ppermute(band[256:], 'seq', up)  8.33 us
    pallas_call x1, Pallas kernels, pack(): pl.pallas_call(pack_kernel, grid=(8,), in_specs=[pl.BlockSpec((1, TOK), l...  7.8 us
  transfers between devices with their start and end apart: 4, of which 4 were waited for; matrix products, arithmetic and copies ran while one was open for 4% of the time, Pallas kernels for 15%

profile of v1, /device:TPU:8, one launch (start us, length us, event | category | flops | bytes accessed | tf_op | source)
XLA Modules:
  0.0 171.2 jit_solution(57205572113679637)
XLA Ops:
  0.0 7.8 %pack.1 = bf16[64,136,128]{2,1,0:T(8,128)(2,1)} custom-call(s32[1,1024]{1,0:T(1,128)} %bitcast.6, bf16[1024,512]{1,0:T(8,128)(2,1)} %feat_ref.1), custom_call_target="tpu_custom_call" | custom-call | tf_op jit(solution)/shard_map/pack/pallas_call | solution.py:70
  7.8 43.0 %all_to_all.5.msg_ref = bf16[64,136,128]{2,1,0:T(8,128)(2,1)} all-to-all(bf16[64,136,128]{2,1,0:T(8,128)(2,1)} %pack.1), channel_id=1, replica_groups=mesh['seq'=64,'head'=2] {'seq'}, dimensions={0} | all-to-all | bytes 4456448 | tf_op jit(solution)/shard_map/all_to_all | solution.py:290
  50.8 5.3 %place.1.band_ref = bf16[1024,512]{1,0:T(8,128)(2,1)} custom-call(bf16[64,136,128]{2,1,0:T(8,128)(2,1)} %all_to_all.5.msg_ref), custom_call_target="tpu_custom_call" | custom-call | tf_op jit(solution)/shard_map/place/pallas_call | solution.py:107
  56.1 0.0 copy-start.5
  56.1 0.0 copy-start.2
  56.1 0.0 copy-start.3
  56.1 0.0 copy-start.4
  56.1 1.5 fusion
  57.6 3.5 %collective-permute-start.1 = (bf16[768,512]{1,0:T(8,128)(2,1)S(1)}, bf16[768,512]{1,0:T(8,128)(2,1)S(1)}, u32[]{:S(2)}, u32[]{:S(2)}) collective-permute-start(bf16[768,512]{1,0:T(8,128)(2,1)S(1)} %get-tuple-element.11), channel_id=1, source_target_pairs={{2,0},{4,2},{6,4},{8,6},{10,8},{12,10},{14,12},{16,14},{18,16},{20... | collective-permute-start | bytes 2359304 | tf_op jit(solution)/shard_map/ppermute | solution.py:295
  61.1 1.9 %collective-permute-start = (bf16[768,512]{1,0:T(8,128)(2,1)S(1)}, bf16[768,512]{1,0:T(8,128)(2,1)S(1)}, u32[]{:S(2)}, u32[]{:S(2)}) collective-permute-start(bf16[768,512]{1,0:T(8,128)(2,1)S(1)} %get-tuple-element.12), channel_id=1, source_target_pairs={{0,2},{2,4},{4,6},{6,8},{8,10},{10,12},{12,14},{14,16},{16,18},{18... | collective-permute-start | bytes 2359304 | tf_op jit(solution)/shard_map/ppermute | solution.py:294
  63.1 0.0 copy-done.5
  63.1 0.6 reshape.28
  63.7 0.0 copy-done.2
  63.7 0.0 copy-done.3
  63.7 0.0 copy-done.4
  63.8 0.7 broadcast_add_fusion.w_ref
  64.5 6.1 %collective-permute-done.1.below_ref = bf16[768,512]{1,0:T(8,128)(2,1)S(1)} collective-permute-done((bf16[768,512]{1,0:T(8,128)(2,1)S(1)}, bf16[768,512]{1,0:T(8,128)(2,1)S(1)}, u32[]{:S(2)}, u32[]{:S(2)}) %collective-permute-start.1) | collective-permute-done | bytes 786464 | tf_op jit(solution)/shard_map/ppermute | solution.py:295
  70.6 8.3 %collective-permute-done.above_ref = bf16[768,512]{1,0:T(8,128)(2,1)S(1)} collective-permute-done((bf16[768,512]{1,0:T(8,128)(2,1)S(1)}, bf16[768,512]{1,0:T(8,128)(2,1)S(1)}, u32[]{:S(2)}, u32[]{:S(2)}) %collective-permute-start) | collective-permute-done | bytes 786464 | tf_op jit(solution)/shard_map/ppermute | solution.py:294
  79.0 0.0 copy-done
  79.0 0.9 copy-done.1
  79.9 11.5 %conv.1.own_ref = bf16[1024,512]{1,0:T(8,128)(2,1)} custom-call(bf16[1024,512]{1,0:T(8,128)(2,1)} %place.1.band_ref, bf16[768,512]{1,0:T(8,128)(2,1)} %copy-done.1, bf16[768,512]{1,0:T(8,128)(2,1)} %copy-done, f32[49,512]{1,0:T(8,128)} %broadcast_add_fusion.w_ref, f32[1,512]{1,0:T(1,128)} %bitcast.5), custom_call_target="tpu_custom_call" | custom-call | tf_op jit(solution)/shard_map/conv/pallas_call | solution.py:157
  91.4 0.6 collective-permute-start.2
  92.0 3.2 %copy.9 = bf16[1024,3,512]{0,2,1:T(8,128)(2,1)S(1)} copy(bf16[1024,3,512]{2,0,1:T(8,128)(2,1)} %param.13) | data formatting | bytes 6291456 | tf_op args[6]
  95.2 3.0 %copy.10.w_own_ref.w_other_ref = bf16[1024,1536]{1,0:T(8,128)(2,1)} copy(bf16[1024,1536]{0,1:T(8,128)(2,1)S(1)} %bitcast.4) | data formatting | bytes 6291456 | tf_op jit(solution)/shard_map/reshape | solution.py:299
  98.1 11.9 %collective-permute-done.2.other_ref = bf16[1024,512]{1,0:T(8,128)(2,1)} collective-permute-done((bf16[1024,512]{1,0:T(8,128)(2,1)}, bf16[1024,512]{1,0:T(8,128)(2,1)}, u32[]{:S(2)}, u32[]{:S(2)}) %collective-permute-start.2) | collective-permute-done | bytes 1048608 | tf_op jit(solution)/shard_map/ppermute | solution.py:298
  110.0 9.0 %project.3.k_ref.v_ref = bf16[1024,1024]{1,0:T(8,128)(2,1)} custom-call(s32[1]{0:T(128)} %bitcast.half_ref, bf16[1024,512]{1,0:T(8,128)(2,1)} %conv.1.own_ref, bf16[1024,512]{1,0:T(8,128)(2,1)} %collective-permute-done.2.other_ref, bf16[1024,1536]{1,0:T(8,128)(2,1)} %copy.10.w_own_ref.w_other_ref, bf16[1024,1536]{1,0:T(8,128)(2,1)} %copy.10.w_own_ref.w_other_ref), custom_call_target="tpu_custom_call" | custom-call | flops 2147483648 | bytes 6291456 | tf_op jit(solution)/shard_map/project/pallas_call | solution.py:188
  119.0 0.0 collective-permute-start.3
  119.0 4.8 %project.2.q_ref = bf16[1024,512]{1,0:T(8,128)(2,1)} custom-call(s32[1]{0:T(128)} %bitcast.half_ref, bf16[1024,512]{1,0:T(8,128)(2,1)} %conv.1.own_ref, bf16[1024,512]{1,0:T(8,128)(2,1)} %collective-permute-done.2.other_ref, bf16[1024,1536]{1,0:T(8,128)(2,1)} %copy.10.w_own_ref.w_other_ref, bf16[1024,1536]{1,0:T(8,128)(2,1)} %copy.10.w_own_ref.w_other_ref), custom_call_target="tpu_custom_call" | custom-call | flops 1073741824 | bytes 4194304 | tf_op jit(solution)/shard_map/project/pallas_call | solution.py:188
  123.8 20.3 %own_keys.1 = (f32[1024,512]{1,0:T(8,128)}, f32[1024,512]{1,0:T(8,128)}, f32[1024,512]{1,0:T(8,128)}) custom-call(bf16[1024,512]{1,0:T(8,128)(2,1)} %project.2.q_ref, bf16[1024,1024]{1,0:T(8,128)(2,1)} %project.3.k_ref.v_ref, bf16[1024,1024]{1,0:T(8,128)(2,1)} %project.3.k_ref.v_ref), custom_call_target="tpu_custom_call" | custom-call | flops 2147483648 | bytes 10485760 | tf_op jit(solution)/shard_map/own_keys/pallas_call | solution.py:259
  144.2 5.1 %collective-permute-done.3.k_ref.v_ref = bf16[1024,1024]{1,0:T(8,128)(2,1)S(1)} collective-permute-done((bf16[1024,1024]{1,0:T(8,128)(2,1)}, bf16[1024,1024]{1,0:T(8,128)(2,1)S(1)}, u32[]{:S(2)}, u32[]{:S(2)}) %collective-permute-start.3) | collective-permute-done | bytes 2097184 | tf_op jit(solution)/shard_map/ppermute | solution.py:302
  149.2 1.3 copy-done.6
  150.5 20.7 %prior_keys.1 = bf16[1024,512]{1,0:T(8,128)(2,1)} custom-call(bf16[1024,512]{1,0:T(8,128)(2,1)} %project.2.q_ref, bf16[1024,1024]{1,0:T(8,128)(2,1)} %copy-done.6, bf16[1024,1024]{1,0:T(8,128)(2,1)} %copy-done.6, f32[1024,512]{1,0:T(8,128)} %get-tuple-element.8.acc_ref, f32[1024,512]{1,0:T(8,128)} %get-tuple-element.9.sum_ref, ...), custom_call_target="tpu_custom_call" | custom-call | flops 2147483648 | bytes 10485760 | tf_op jit(solution)/shard_map/prior_keys/pallas_call | solution.py:269
  (6 shorter events, 0.1 us)
Async XLA Ops:
  56.1 7.0 %copy-start.5 = (bf16[512]{0:T(512)(128)(2,1)S(1)}, bf16[512]{0:T(512)(128)(2,1)}, u32[]{:S(2)}) copy-start(bf16[512]{0:T(512)(128)(2,1)} %param.12) | copy-start | bytes 3076
  56.1 7.6 %copy-start.2 = (bf16[7,7,512]{2,1,0:T(8,128)(2,1)S(1)}, bf16[7,7,512]{2,1,0:T(8,128)(2,1)}, u32[]{:S(2)}) copy-start(bf16[7,7,512]{2,1,0:T(8,128)(2,1)} %param.9) | copy-start | bytes 150532
  56.1 7.6 %copy-start.3 = (bf16[5,5,512]{2,1,0:T(8,128)(2,1)S(1)}, bf16[5,5,512]{2,1,0:T(8,128)(2,1)}, u32[]{:S(2)}) copy-start(bf16[5,5,512]{2,1,0:T(8,128)(2,1)} %param.10) | copy-start | bytes 76804
  56.1 7.6 %copy-start.4 = (bf16[3,3,512]{2,1,0:T(4,128)(2,1)S(1)}, bf16[3,3,512]{2,1,0:T(4,128)(2,1)}, u32[]{:S(2)}) copy-start(bf16[3,3,512]{2,1,0:T(4,128)(2,1)} %param.11) | copy-start | bytes 27652
  57.6 13.0 %collective-permute-start.1 = (bf16[768,512]{1,0:T(8,128)(2,1)S(1)}, bf16[768,512]{1,0:T(8,128)(2,1)S(1)}, u32[]{:S(2)}, u32[]{:S(2)}) collective-permute-start(bf16[768,512]{1,0:T(8,128)(2,1)S(1)} %get-tuple-element.11), channel_id=1, source_target_pairs={{2,0},{4,2},{6,4},{8,6},{10,8},{12,10},{14,12},{16,14},{18,16},{20... | collective-permute-start | bytes 2359304 | tf_op jit(solution)/shard_map/ppermute | solution.py:295
  61.1 17.8 %collective-permute-start = (bf16[768,512]{1,0:T(8,128)(2,1)S(1)}, bf16[768,512]{1,0:T(8,128)(2,1)S(1)}, u32[]{:S(2)}, u32[]{:S(2)}) collective-permute-start(bf16[768,512]{1,0:T(8,128)(2,1)S(1)} %get-tuple-element.12), channel_id=1, source_target_pairs={{0,2},{2,4},{4,6},{6,8},{8,10},{10,12},{12,14},{14,16},{16,18},{18... | collective-permute-start | bytes 2359304 | tf_op jit(solution)/shard_map/ppermute | solution.py:294
  70.6 8.3 %copy-start = (bf16[768,512]{1,0:T(8,128)(2,1)}, bf16[768,512]{1,0:T(8,128)(2,1)S(1)}, u32[]{:S(2)}) copy-start(bf16[768,512]{1,0:T(8,128)(2,1)S(1)} %collective-permute-done.1.below_ref) | copy-start | bytes 2359300
  79.0 0.9 copy-start.1
  91.4 18.6 %collective-permute-start.2 = (bf16[1024,512]{1,0:T(8,128)(2,1)}, bf16[1024,512]{1,0:T(8,128)(2,1)}, u32[]{:S(2)}, u32[]{:S(2)}) collective-permute-start(bf16[1024,512]{1,0:T(8,128)(2,1)} %conv.1.own_ref), channel_id=1, source_target_pairs={{0,1},{1,0},{2,3},{3,2},{4,5},{5,4},{6,7},{7,6},{8,9},{9,8},{10,11... | collective-permute-start | bytes 3145736 | tf_op jit(solution)/shard_map/ppermute | solution.py:298
  119.0 30.2 %collective-permute-start.3 = (bf16[1024,1024]{1,0:T(8,128)(2,1)}, bf16[1024,1024]{1,0:T(8,128)(2,1)S(1)}, u32[]{:S(2)}, u32[]{:S(2)}) collective-permute-start(bf16[1024,1024]{1,0:T(8,128)(2,1)} %project.3.k_ref.v_ref), channel_id=1, source_target_pairs={{0,2},{2,4},{4,6},{6,8},{8,10},{10,12},{12,14},{14,16},{16,18},{18... | collective-permute-start | bytes 6291464 | tf_op jit(solution)/shard_map/ppermute | solution.py:302
  149.2 1.3 copy-start.6

commit v2 on v1

v2 whole, which is shorter than its diff:
```python
import functools
import math

import jax
import jax.numpy as jnp
from jax import lax
from jax.experimental import pallas as pl
from jax.experimental.pallas import tpu as pltpu
from jax.sharding import PartitionSpec as P

D = 1024
HEADS = 16
GRID_W = 256
BANDS = 64
TOK = 1024
LOCAL = 512
CAP = 32
MSG = 4 * CAP + 8
BF16 = jnp.bfloat16
F32 = jnp.float32
VMEM_BYTES = 56 * 1024 * 1024


def iota(shape, dim):
    return lax.broadcasted_iota(jnp.int32, shape, dim)


def ones_where(mask):
    return jnp.where(mask, 1.0, 0.0).astype(BF16)


def params(**kwargs):
    return pltpu.CompilerParams(vmem_limit_bytes=VMEM_BYTES, **kwargs)


def pack_kernel(cells_ref, feat_ref, out_ref, slot_ref, info_ref):
    step = pl.program_id(0)

    @pl.when(step == 0)
    def _():
        cells = cells_ref[...]
        band = cells >> 10
        within = cells & (TOK - 1)
        member = jnp.where(iota((BANDS, TOK), 0) == band, 1.0, 0.0)
        before = ones_where(iota((TOK, TOK), 0) < iota((TOK, TOK), 1))
        counts = jnp.dot(member.astype(BF16), before, preferred_element_type=F32)
        rank = jnp.sum(member * counts, axis=0, keepdims=True).astype(jnp.int32)
        slot_ref[...] = band * CAP + rank
        place = (within & 768) | ((within & 31) << 3) | ((within >> 5) & 7)
        row = iota((16, TOK), 0)
        info = jnp.where(row == 0, (place >> 5) + 1, jnp.where(row == 1, place & 31, 0))
        info_ref[...] = info.astype(F32).astype(BF16)

    chosen = ones_where(slot_ref[...] - step * 256 == iota((256, TOK), 0))
    rows = jnp.dot(chosen, feat_ref[...], preferred_element_type=F32).astype(BF16)
    for c in range(4):
        out_ref[:, c * CAP : (c + 1) * CAP, :] = rows[:, c * 128 : (c + 1) * 128].reshape(8, CAP, 128)
    info = lax.dot_general(
        info_ref[...], chosen, (((1,), (1,)), ((), ())), preferred_element_type=F32
    )
    group = iota((8, 128), 1) // CAP
    for d in range(8):
        own = jnp.where(group == d % 4, info[:8, d // 4 * 128 : d // 4 * 128 + 128], 0.0)
        own = own + pltpu.roll(own, 64, 1)
        own = own + pltpu.roll(own, 32, 1)
        out_ref[d, 4 * CAP :, :] = own.astype(BF16)


def pack(cells, features):
    return pl.pallas_call(
        pack_kernel,
        grid=(8,),
        in_specs=[
            pl.BlockSpec((1, TOK), lambda i: (0, 0)),
            pl.BlockSpec((TOK, LOCAL), lambda i: (0, 0)),
        ],
        out_specs=pl.BlockSpec((8, MSG, 128), lambda i: (i, 0, 0)),
        out_shape=jax.ShapeDtypeStruct((BANDS, MSG, 128), BF16),
        scratch_shapes=[pltpu.VMEM((1, TOK), jnp.int32), pltpu.VMEM((16, TOK), BF16)],
        compiler_params=params(),
        name="pack",
    )(cells.reshape(1, TOK), features)


def place_kernel(msg_ref, first_ref, last_ref, place_ref):
    step = pl.program_id(0)

    @pl.when(step == 0)
    def _():
        info = msg_ref[:, 4 * CAP :, :].astype(F32).reshape(16, 4, 8, 128)
        shape = (16, 4, 8, 128)
        info = jnp.sum(jnp.where(iota(shape, 3) // CAP == iota(shape, 1), info, 0.0), axis=1)
        place_ref[...] = (info[:, 0, :] * 32.0 + info[:, 1, :]).astype(jnp.int32) - 32

    cell = iota((256, 128), 0) + step * 256
    chosen = jnp.concatenate(
        [ones_where(place_ref[g : g + 1, :] == cell) for g in range(16)], axis=1
    )
    rows = jnp.concatenate(
        [msg_ref[:, c * CAP : (c + 1) * CAP, :].reshape(BANDS * CAP, 128) for c in range(4)],
        axis=1,
    )
    row = jnp.dot(chosen, rows, preferred_element_type=F32).astype(BF16)

    @pl.when(step < 3)
    def _():
        first_ref[...] = row

    @pl.when(step > 0)
    def _():
        last_ref[...] = row


def place(messages):
    return pl.pallas_call(
        place_kernel,
        grid=(4,),
        in_specs=[pl.BlockSpec((BANDS, MSG, 128), lambda i: (0, 0, 0))],
        out_specs=[
            pl.BlockSpec((256, LOCAL), lambda i: (jnp.minimum(i, 2), 0)),
            pl.BlockSpec((256, LOCAL), lambda i: (jnp.maximum(i - 1, 0), 0)),
        ],
        out_shape=[jax.ShapeDtypeStruct((768, LOCAL), BF16)] * 2,
        scratch_shapes=[pltpu.VMEM((16, 128), jnp.int32)],
        compiler_params=params(),
        name="place",
    )(messages)


def conv_kernel(far_ref, first_ref, last_ref, near_ref, w_ref, bias_ref, out_ref, x_ref, tap_ref, nat_ref, *, upper):
    sub = iota((3, 8, 128), 1)
    own = [(first_ref, 0), (first_ref, 1), (first_ref, 2), (last_ref, 2)]
    far = [(far_ref, r) for r in range(3)]
    sources = far + own + [(near_ref, 0)] if upper else [(near_ref, 0)] + own + far
    for r, (ref, at) in enumerate(sources):
        x = ref[at * 256 : (at + 1) * 256, :].astype(F32).reshape(32, 8, 128)
        x_ref[r, 3:35] = x
        x_ref[r, 0:3] = jnp.where(sub == 0, 0.0, pltpu.roll(x[29:32], 1, 1))
        x_ref[r, 35:38] = jnp.where(sub == 7, 0.0, pltpu.roll(x[0:3], 7, 1))
    for t in range(49):
        tap_ref[t] = jnp.broadcast_to(w_ref[t : t + 1, :], (8, 128))
    bias = jnp.broadcast_to(bias_ref[...], (8, 128))

    def group(g, carry):
        k = g * KGROUP
        acc = [[bias] * KGROUP for _ in range(2)]
        for j in range(7):
            for r in range(8):
                taps = [tap_ref[(r - o) * 7 + j] if 0 <= r - o < 7 else None for o in range(2)]
                for n in range(KGROUP):
                    x = x_ref[r, k + j + n]
                    for o in range(2):
                        if taps[o] is not None:
                            acc[o][n] = acc[o][n] + x * taps[o]
        for o in range(2):
            for n in range(KGROUP):
                nat_ref[pl.ds(o * 256 + k + n, 8, stride=32), :] = acc[o][n]
        return carry

    lax.fori_loop(0, 32 // KGROUP, group, 0)
    out_ref[...] = nat_ref[...].astype(BF16)


KGROUP = 8


def conv(first, last, above, below, taps, bias, upper):
    column = lambda rows, at=0: pl.BlockSpec((rows, 128), lambda i: (at, i))
    far, near = (above, below) if upper else (below, above)
    return pl.pallas_call(
        functools.partial(conv_kernel, upper=upper),
        grid=(4,),
        in_specs=[
            column(768), column(768), column(768), column(256, 0 if upper else 2), column(49), column(1),
        ],
        out_specs=column(512),
        out_shape=jax.ShapeDtypeStruct((512, LOCAL), BF16),
        scratch_shapes=[
            pltpu.VMEM((8, 38, 8, 128), F32),
            pltpu.VMEM((49, 8, 128), F32),
            pltpu.VMEM((512, 128), F32),
        ],
        compiler_params=params(),
        cost_estimate=pl.CostEstimate(flops=98 * 512 * LOCAL, bytes_accessed=4 * 2**20, transcendentals=0),
        name="conv_upper" if upper else "conv_lower",
    )(far, first, last, near, taps, bias)


def project_kernel(half_ref, own_ref, other_ref, w_own_ref, w_other_ref, kv_ref, q_ref):
    step = pl.program_id(0)
    out = (
        jnp.dot(own_ref[...], w_own_ref[...], preferred_element_type=F32)
        + jnp.dot(other_ref[...], w_other_ref[...], preferred_element_type=F32)
    ).astype(BF16)

    @pl.when(step < 2)
    def _():
        kv_ref[...] = out

    @pl.when(step == 2)
    def _():
        q_ref[...] = out


def project(half, own, other, weights):
    rows = own.shape[0]
    third = lambda j: jnp.where(j == 2, 0, j + 1)
    return pl.pallas_call(
        project_kernel,
        grid_spec=pltpu.PrefetchScalarGridSpec(
            num_scalar_prefetch=1,
            grid=(3,),
            in_specs=[
                pl.BlockSpec((rows, LOCAL), lambda j, h: (0, 0)),
                pl.BlockSpec((rows, LOCAL), lambda j, h: (0, 0)),
                pl.BlockSpec((LOCAL, LOCAL), lambda j, h: (h[0], third(j))),
                pl.BlockSpec((LOCAL, LOCAL), lambda j, h: (1 - h[0], third(j))),
            ],
            out_specs=[
                pl.BlockSpec((rows, LOCAL), lambda j, h: (0, jnp.minimum(j, 1))),
                pl.BlockSpec((rows, LOCAL), lambda j, h: (0, 0)),
            ],
        ),
        out_shape=[
            jax.ShapeDtypeStruct((rows, 2 * LOCAL), BF16),
            jax.ShapeDtypeStruct((rows, LOCAL), BF16),
        ],
        compiler_params=params(),
        cost_estimate=pl.CostEstimate(
            flops=2 * rows * D * 3 * LOCAL, bytes_accessed=6 * 2**20, transcendentals=0
        ),
        name="project",
    )(half, own, other, weights, weights)


def partial_attention(queries, keys, values):
    v = jnp.concatenate([values, jnp.ones(values.shape, BF16)], axis=1)
    lane = iota(queries[0].shape, 1)

    def scores(step):
        mine = (lane // 64) == step % 2
        return lax.dot_general(
            jnp.where(mine, queries[step // 2] * 0.125, 0.0).astype(BF16),
            keys,
            (((1,), (1,)), ((), ())),
            preferred_element_type=F32,
        )

    ready, parts = scores(0), []
    for step in range(2 * len(queries)):
        current = ready
        if step + 1 < 2 * len(queries):
            ready = scores(step + 1)
        top = jnp.max(current, axis=1, keepdims=True)
        weight = jnp.exp(current - top).astype(BF16)
        summed = jnp.dot(weight, v, preferred_element_type=F32)
        parts.append((summed[:, :128], summed[:, 128:], jnp.broadcast_to(top, lane.shape)))
        if step % 2:
            yield [jnp.where(lane < 64, a, b) for a, b in zip(*parts)]
            parts = []


QROWS = 256


def blocks_of(*refs):
    return [
        (ref[r : r + QROWS, :]) for ref in refs for r in range(0, ref.shape[0], QROWS)
    ]


def stacked(*refs):
    return jnp.concatenate([ref[...] for ref in refs], axis=0)


def own_kernel(q0_ref, q1_ref, k0_ref, k1_ref, v0_ref, v1_ref, acc_ref, sum_ref, top_ref):
    parts = partial_attention(
        blocks_of(q0_ref, q1_ref), stacked(k0_ref, k1_ref), stacked(v0_ref, v1_ref)
    )
    for i, (acc, total, top) in enumerate(parts):
        rows = slice(i * QROWS, (i + 1) * QROWS)
        acc_ref[rows, :], sum_ref[rows, :], top_ref[rows, :] = acc, total, top


def prior_kernel(
    q0_ref, q1_ref, k0_ref, k1_ref, v0_ref, v1_ref, acc_ref, sum_ref, top_ref, out_ref
):
    parts = partial_attention(
        blocks_of(q0_ref, q1_ref), stacked(k0_ref, k1_ref), stacked(v0_ref, v1_ref)
    )
    for i, (acc, total, top) in enumerate(parts):
        rows = slice(i * QROWS, (i + 1) * QROWS)
        highest = jnp.maximum(top, top_ref[rows, :])
        here, there = jnp.exp(top - highest), jnp.exp(top_ref[rows, :] - highest)
        total = total * here + sum_ref[rows, :] * there
        out_ref[rows, :] = ((acc * here + acc_ref[rows, :] * there) / total).astype(BF16)


def attend(queries, keys_values, state=None):
    column = lambda rows, first=0: pl.BlockSpec((rows, 128), lambda p: (0, first + p))
    in_specs = [column(512)] * 4 + [column(512, 4)] * 2
    cost = pl.CostEstimate(
        flops=4 * TOK * TOK * LOCAL, bytes_accessed=10 * 2**20, transcendentals=8 * TOK * TOK
    )
    if state is None:
        return pl.pallas_call(
            own_kernel,
            grid=(4,),
            in_specs=in_specs,
            out_specs=[column(TOK)] * 3,
            out_shape=[jax.ShapeDtypeStruct((TOK, LOCAL), F32)] * 3,
            compiler_params=params(),
            cost_estimate=cost,
            name="own_keys",
        )(*queries, *keys_values, *keys_values)
    return pl.pallas_call(
        prior_kernel,
        grid=(4,),
        in_specs=in_specs + [column(TOK)] * 3,
        out_specs=column(TOK),
        out_shape=jax.ShapeDtypeStruct((TOK, LOCAL), BF16),
        compiler_params=params(),
        cost_estimate=cost,
        name="prior_keys",
    )(*queries, *keys_values, *keys_values, *state)


def merged_taps(conv7, conv5, conv3):
    taps = conv7.astype(F32)
    taps = taps + jnp.pad(conv5.astype(F32), ((1, 1), (1, 1), (0, 0)))
    taps = taps + jnp.pad(conv3.astype(F32), ((2, 2), (2, 2), (0, 0)))
    return taps.reshape(49, LOCAL) + (jnp.arange(49) == 24).astype(F32)[:, None]


def shards(features, cells, conv7, conv5, conv3, conv_bias, w_qkv):
    messages = pack(cells, features)
    arrived = lax.all_to_all(messages, "seq", split_axis=0, concat_axis=0, tiled=True)
    first, last = place(arrived)
    up = [(i, i + 1) for i in range(BANDS - 1)]
    down = [(j, i) for i, j in up]
    above = lax.ppermute(last, "seq", up)
    below = lax.ppermute(first, "seq", down)
    taps = merged_taps(conv7, conv5, conv3)
    bias = conv_bias.astype(F32).reshape(1, LOCAL)
    weights = w_qkv.reshape(D, 3 * LOCAL)
    half = lax.axis_index("head").astype(jnp.int32).reshape(1)
    ring = [(i, (i + 1) % BANDS) for i in range(BANDS)]
    mixed = [conv(first, last, above, below, taps, bias, upper) for upper in (True, False)]
    others = [lax.ppermute(own, "head", [(0, 1), (1, 0)]) for own in mixed]
    keys_values, queries = zip(
        *[project(half, own, other, weights) for own, other in zip(mixed, others)]
    )
    prior = [lax.ppermute(block, "seq", ring) for block in keys_values]
    state = attend(queries, keys_values)
    return attend(queries, prior, state)


def solution(mesh):
    placed = (
        P("seq", "head"),
        P("seq"),
        P(None, None, "head"),
        P(None, None, "head"),
        P(None, None, "head"),
        P("head"),
        P(None, None, "head"),
    )
    return jax.shard_map(
        shards, mesh=mesh, in_specs=placed, out_specs=P("seq", "head"), check_vma=False
    )
```

time: 172 us -> 150 us (0.87)
  Pallas kernels: 79.4 us -> 64.4 us
  waiting for transfers between devices: 31.4 us -> 20.1 us
  starting transfers between devices: 6.06 us -> 12.1 us
  local copies, waits for them, and re-layouts: 9.88 us -> 8.08 us
    pallas_call x3 -> x4, Pallas kernels: 52.5 us -> 40 us  [the longest x1 13.8 us: attend(): pl.pallas_call(prior_kernel, grid=(4,), in_specs=in_specs + [column(TOK)]...]
    ppermute x4 -> x6, waiting for transfers between devices: 31.4 us -> 20.1 us  [the longest x2 10 us: shards(): prior = [lax.ppermute(block, 'seq', ring) for block in keys_values]]
    ppermute x4 -> x6, starting transfers between devices: 6.06 us -> 12.1 us  [the longest x1 8.05 us: shards(): below = lax.ppermute(first, 'seq', down)]
    pallas_call x2, Pallas kernels: 13.8 us -> 10.9 us  [project(): pl.pallas_call(project_kernel, grid_spec=pltpu.PrefetchScalarGridSpec(num...]
    unnamed x15 -> x17, local copies, waits for them, and re-layouts: 5.39 us -> 5.1 us
  transfers between devices with their start and end apart: 4 -> 6, of which waited for: 4 -> 5; matrix products, arithmetic and copies ran while one was open for 4% -> 5% of each run, Pallas kernels for 15% -> 21%
where the time goes in v2:
time: 150 us; the launch traced here: 149 us
  Pallas kernels  64.4 us (43%)
  blocking collectives  43 us (29%)
  waiting for transfers between devices  20.1 us (13%)
  starting transfers between devices  12.1 us (8%)
  local copies, waits for them, and re-layouts  8.08 us (5%)
    all_to_all x1, blocking collectives, shards(): lax.all_to_all(messages, 'seq', split_axis=0, concat_axis=0, tiled=True)  43 us
    pallas_call x1, Pallas kernels, attend(): pl.pallas_call(prior_kernel, grid=(4,), in_specs=in_specs + [column(TOK)]...  13.8 us
    pallas_call x1, Pallas kernels, attend(): pl.pallas_call(own_kernel, grid=(4,), in_specs=in_specs, out_specs=[colum...  13.6 us
    pallas_call x2, Pallas kernels, conv(): pl.pallas_call(functools.partial(conv_kernel, upper=upper), grid=(4,), in...  12.6 us
    pallas_call x2, Pallas kernels, project(): pl.pallas_call(project_kernel, grid_spec=pltpu.PrefetchScalarGridSpec(num...  10.9 us
    ppermute x2, waiting for transfers between devices, shards(): prior = [lax.ppermute(block, 'seq', ring) for block in keys_values]  10 us
    ppermute x1, starting transfers between devices, shards(): below = lax.ppermute(first, 'seq', down)  8.05 us
    pallas_call x1, Pallas kernels, pack(): pl.pallas_call(pack_kernel, grid=(8,), in_specs=[pl.BlockSpec((1, TOK), l...  7.83 us
  transfers between devices with their start and end apart: 6, of which 5 were waited for; matrix products, arithmetic and copies ran while one was open for 5% of the time, Pallas kernels for 21%

profile of v2, /device:TPU:8, one launch (start us, length us, event | category | flops | bytes accessed | tf_op | source)
XLA Modules:
  0.0 149.2 jit_solution(7799419496562786796)
XLA Ops:
  0.0 7.8 %pack.1 = bf16[64,136,128]{2,1,0:T(8,128)(2,1)} custom-call(s32[1,1024]{1,0:T(1,128)} %bitcast.7, bf16[1024,512]{1,0:T(8,128)(2,1)} %feat_ref.1), custom_call_target="tpu_custom_call" | custom-call | tf_op jit(solution)/shard_map/pack/pallas_call | solution.py:70
  7.8 43.0 %all_to_all.5.msg_ref = bf16[64,136,128]{2,1,0:T(8,128)(2,1)} all-to-all(bf16[64,136,128]{2,1,0:T(8,128)(2,1)} %pack.1), channel_id=1, replica_groups=mesh['seq'=64,'head'=2] {'seq'}, dimensions={0} | all-to-all | bytes 4456448 | tf_op jit(solution)/shard_map/all_to_all | solution.py:337
  50.8 5.6 %place.1 = (bf16[768,512]{1,0:T(8,128)(2,1)}, bf16[768,512]{1,0:T(8,128)(2,1)}) custom-call(bf16[64,136,128]{2,1,0:T(8,128)(2,1)} %all_to_all.5.msg_ref), custom_call_target="tpu_custom_call" | custom-call | tf_op jit(solution)/shard_map/place/pallas_call | solution.py:115
  56.4 2.0 %collective-permute-start = (bf16[768,512]{1,0:T(8,128)(2,1)}, bf16[768,512]{1,0:T(8,128)(2,1)S(1)}, u32[]{:S(2)}, u32[]{:S(2)}) collective-permute-start(bf16[768,512]{1,0:T(8,128)(2,1)} %get-tuple-element.14.last_ref), channel_id=1, source_target_pairs={{0,2},{2,4},{4,6},{6,8},{8,10},{10,12},{12,14},{14,16},{16,18},{18... | collective-permute-start | bytes 2359304 | tf_op jit(solution)/shard_map/ppermute | solution.py:341
  58.5 8.0 %collective-permute-start.1 = (bf16[768,512]{1,0:T(8,128)(2,1)}, bf16[768,512]{1,0:T(8,128)(2,1)S(1)}, u32[]{:S(2)}, u32[]{:S(2)}) collective-permute-start(bf16[768,512]{1,0:T(8,128)(2,1)} %get-tuple-element.15.first_ref), channel_id=1, source_target_pairs={{2,0},{4,2},{6,4},{8,6},{10,8},{12,10},{14,12},{16,14},{18,16},{20... | collective-permute-start | bytes 2359304 | tf_op jit(solution)/shard_map/ppermute | solution.py:342
  66.5 0.0 copy-done.2
  66.5 0.0 copy-done.3
  66.5 0.0 copy-done.4
  66.6 0.0 copy-done.5
  66.6 0.6 reshape.28
  67.2 0.7 broadcast_add_fusion.w_ref
  67.9 6.5 %collective-permute-done.far_ref.near_ref = bf16[768,512]{1,0:T(8,128)(2,1)S(1)} collective-permute-done((bf16[768,512]{1,0:T(8,128)(2,1)}, bf16[768,512]{1,0:T(8,128)(2,1)S(1)}, u32[]{:S(2)}, u32[]{:S(2)}) %collective-permute-start) | collective-permute-done | bytes 786464 | tf_op jit(solution)/shard_map/ppermute | solution.py:341
  74.5 1.9 %collective-permute-done.1.near_ref.far_ref = bf16[768,512]{1,0:T(8,128)(2,1)S(1)} collective-permute-done((bf16[768,512]{1,0:T(8,128)(2,1)}, bf16[768,512]{1,0:T(8,128)(2,1)S(1)}, u32[]{:S(2)}, u32[]{:S(2)}) %collective-permute-start.1) | collective-permute-done | bytes 786464 | tf_op jit(solution)/shard_map/ppermute | solution.py:342
  76.3 0.0 copy-done
  76.3 0.9 copy-done.1
  77.2 6.3 %conv_lower.1.own_ref = bf16[512,512]{1,0:T(8,128)(2,1)} custom-call(bf16[768,512]{1,0:T(8,128)(2,1)} %copy-done.1, bf16[768,512]{1,0:T(8,128)(2,1)} %get-tuple-element.15.first_ref, bf16[768,512]{1,0:T(8,128)(2,1)} %get-tuple-element.14.last_ref, bf16[768,512]{1,0:T(8,128)(2,1)} %copy-done, f32[49,512]{1,0:T(8,128)} %broadcast_add_fusion.w_ref, ...), custom_call_target="tpu_custom_call" | custom-call | flops 25690112 | bytes 4194304 | tf_op jit(solution)/shard_map/conv_lower/pallas_call | solution.py:170
  83.5 0.6 collective-permute-start.3
  84.1 6.3 %conv_upper.1.own_ref = bf16[512,512]{1,0:T(8,128)(2,1)} custom-call(bf16[768,512]{1,0:T(8,128)(2,1)} %copy-done, bf16[768,512]{1,0:T(8,128)(2,1)} %get-tuple-element.15.first_ref, bf16[768,512]{1,0:T(8,128)(2,1)} %get-tuple-element.14.last_ref, bf16[768,512]{1,0:T(8,128)(2,1)} %copy-done.1, f32[49,512]{1,0:T(8,128)} %broadcast_add_fusion.w_ref, ...), custom_call_target="tpu_custom_call" | custom-call | flops 25690112 | bytes 4194304 | tf_op jit(solution)/shard_map/conv_upper/pallas_call | solution.py:170
  90.4 1.4 collective-permute-start.2
  91.9 3.2 %copy.9 = bf16[1024,3,512]{0,2,1:T(8,128)(2,1)S(1)} copy(bf16[1024,3,512]{2,0,1:T(8,128)(2,1)} %param.13) | data formatting | bytes 6291456 | tf_op args[6]
  95.1 3.0 %copy.10.w_own_ref.w_other_ref = bf16[1024,1536]{1,0:T(8,128)(2,1)} copy(bf16[1024,1536]{0,1:T(8,128)(2,1)S(1)} %bitcast.4) | data formatting | bytes 6291456 | tf_op jit(solution)/shard_map/reshape | solution.py:345
  98.0 0.6 collective-permute-done.3.other_ref
  98.6 5.5 %project.3 = (bf16[512,1024]{1,0:T(8,128)(2,1)}, bf16[512,512]{1,0:T(8,128)(2,1)}) custom-call(s32[1]{0:T(128)} %bitcast.half_ref, bf16[512,512]{1,0:T(8,128)(2,1)} %conv_lower.1.own_ref, bf16[512,512]{1,0:T(8,128)(2,1)} %collective-permute-done.3.other_ref, bf16[1024,1536]{1,0:T(8,128)(2,1)} %copy.10.w_own_ref.w_other_ref, ...), custom_call_target="tpu_custom_call" | custom-call | flops 1610612736 | bytes 6291456 | tf_op jit(solution)/shard_map/project/pallas_call | solution.py:208
  104.1 0.0 collective-permute-start.5
  104.1 1.1 collective-permute-done.2.other_ref
  105.2 5.4 %project.2 = (bf16[512,1024]{1,0:T(8,128)(2,1)}, bf16[512,512]{1,0:T(8,128)(2,1)}) custom-call(s32[1]{0:T(128)} %bitcast.half_ref, bf16[512,512]{1,0:T(8,128)(2,1)} %conv_upper.1.own_ref, bf16[512,512]{1,0:T(8,128)(2,1)} %collective-permute-done.2.other_ref, bf16[1024,1536]{1,0:T(8,128)(2,1)} %copy.10.w_own_ref.w_other_ref, ...), custom_call_target="tpu_custom_call" | custom-call | flops 1610612736 | bytes 6291456 | tf_op jit(solution)/shard_map/project/pallas_call | solution.py:208
  110.7 0.0 collective-permute-start.4
  110.7 13.6 %own_keys.1 = (f32[1024,512]{1,0:T(8,128)}, f32[1024,512]{1,0:T(8,128)}, f32[1024,512]{1,0:T(8,128)}) custom-call(bf16[512,512]{1,0:T(8,128)(2,1)} %get-tuple-element.16.q0_ref, bf16[512,512]{1,0:T(8,128)(2,1)} %get-tuple-element.17.q1_ref, bf16[512,1024]{1,0:T(8,128)(2,1)} %get-tuple-element.18.k0_ref.v0_ref, ...), custom_call_target="tpu_custom_call" | custom-call | flops 2147483648 | bytes 10485760 | tf_op jit(solution)/shard_map/own_keys/pallas_call | solution.py:306
  124.3 0.0 collective-permute-done.5.k1_ref.v1_ref
  124.3 10.0 %collective-permute-done.4.k0_ref.v0_ref = bf16[512,1024]{1,0:T(8,128)(2,1)S(1)} collective-permute-done((bf16[512,1024]{1,0:T(8,128)(2,1)}, bf16[512,1024]{1,0:T(8,128)(2,1)S(1)}, u32[]{:S(2)}, u32[]{:S(2)}) %collective-permute-start.4) | collective-permute-done | bytes 1048608 | tf_op jit(solution)/shard_map/ppermute | solution.py:353
  134.3 1.0 copy-done.7
  135.3 13.8 %prior_keys.1 = bf16[1024,512]{1,0:T(8,128)(2,1)} custom-call(bf16[512,512]{1,0:T(8,128)(2,1)} %get-tuple-element.16.q0_ref, bf16[512,512]{1,0:T(8,128)(2,1)} %get-tuple-element.17.q1_ref, bf16[512,1024]{1,0:T(8,128)(2,1)} %copy-done.7, bf16[512,1024]{1,0:T(8,128)(2,1)} %copy-done.6, bf16[512,1024]{1,0:T(8,128)(2,1)} %copy-done.7, ...), custom_call_target="tpu_custom_call" | custom-call | flops 2147483648 | bytes 10485760 | tf_op jit(solution)/shard_map/prior_keys/pallas_call | solution.py:316
  (12 shorter events, 0.1 us)
Async XLA Ops:
  50.8 15.7 %copy-start.2 = (bf16[7,7,512]{2,1,0:T(8,128)(2,1)S(1)}, bf16[7,7,512]{2,1,0:T(8,128)(2,1)}, u32[]{:S(2)}) copy-start(bf16[7,7,512]{2,1,0:T(8,128)(2,1)} %param.9) | copy-start | bytes 150532
  50.8 15.7 %copy-start.3 = (bf16[5,5,512]{2,1,0:T(8,128)(2,1)S(1)}, bf16[5,5,512]{2,1,0:T(8,128)(2,1)}, u32[]{:S(2)}) copy-start(bf16[5,5,512]{2,1,0:T(8,128)(2,1)} %param.10) | copy-start | bytes 76804
  50.8 15.7 %copy-start.4 = (bf16[3,3,512]{2,1,0:T(4,128)(2,1)S(1)}, bf16[3,3,512]{2,1,0:T(4,128)(2,1)}, u32[]{:S(2)}) copy-start(bf16[3,3,512]{2,1,0:T(4,128)(2,1)} %param.11) | copy-start | bytes 27652
  50.8 15.8 %copy-start.5 = (bf16[512]{0:T(512)(128)(2,1)S(1)}, bf16[512]{0:T(512)(128)(2,1)}, u32[]{:S(2)}) copy-start(bf16[512]{0:T(512)(128)(2,1)} %param.12) | copy-start | bytes 3076
  56.4 18.0 %collective-permute-start = (bf16[768,512]{1,0:T(8,128)(2,1)}, bf16[768,512]{1,0:T(8,128)(2,1)S(1)}, u32[]{:S(2)}, u32[]{:S(2)}) collective-permute-start(bf16[768,512]{1,0:T(8,128)(2,1)} %get-tuple-element.14.last_ref), channel_id=1, source_target_pairs={{0,2},{2,4},{4,6},{6,8},{8,10},{10,12},{12,14},{14,16},{16,18},{18... | collective-permute-start | bytes 2359304 | tf_op jit(solution)/shard_map/ppermute | solution.py:341
  58.5 17.9 %collective-permute-start.1 = (bf16[768,512]{1,0:T(8,128)(2,1)}, bf16[768,512]{1,0:T(8,128)(2,1)S(1)}, u32[]{:S(2)}, u32[]{:S(2)}) collective-permute-start(bf16[768,512]{1,0:T(8,128)(2,1)} %get-tuple-element.15.first_ref), channel_id=1, source_target_pairs={{2,0},{4,2},{6,4},{8,6},{10,8},{12,10},{14,12},{16,14},{18,16},{20... | collective-permute-start | bytes 2359304 | tf_op jit(solution)/shard_map/ppermute | solution.py:342
  74.5 1.9 %copy-start = (bf16[768,512]{1,0:T(8,128)(2,1)}, bf16[768,512]{1,0:T(8,128)(2,1)S(1)}, u32[]{:S(2)}) copy-start(bf16[768,512]{1,0:T(8,128)(2,1)S(1)} %collective-permute-done.far_ref.near_ref) | copy-start | bytes 2359300
  76.3 0.9 copy-start.1
  83.5 15.1 %collective-permute-start.3 = (bf16[512,512]{1,0:T(8,128)(2,1)}, bf16[512,512]{1,0:T(8,128)(2,1)}, u32[]{:S(2)}, u32[]{:S(2)}) collective-permute-start(bf16[512,512]{1,0:T(8,128)(2,1)} %conv_lower.1.own_ref), channel_id=1, source_target_pairs={{0,1},{1,0},{2,3},{3,2},{4,5},{5,4},{6,7},{7,6},{8,9},{9,8},{10,11... | collective-permute-start | bytes 1572872 | tf_op jit(solution)/shard_map/ppermute | solution.py:349
  90.4 14.8 %collective-permute-start.2 = (bf16[512,512]{1,0:T(8,128)(2,1)}, bf16[512,512]{1,0:T(8,128)(2,1)}, u32[]{:S(2)}, u32[]{:S(2)}) collective-permute-start(bf16[512,512]{1,0:T(8,128)(2,1)} %conv_upper.1.own_ref), channel_id=1, source_target_pairs={{0,1},{1,0},{2,3},{3,2},{4,5},{5,4},{6,7},{7,6},{8,9},{9,8},{10,11... | collective-permute-start | bytes 1572872 | tf_op jit(solution)/shard_map/ppermute | solution.py:349
  104.1 20.1 %collective-permute-start.5 = (bf16[512,1024]{1,0:T(8,128)(2,1)}, bf16[512,1024]{1,0:T(8,128)(2,1)S(1)}, u32[]{:S(2)}, u32[]{:S(2)}) collective-permute-start(bf16[512,1024]{1,0:T(8,128)(2,1)} %get-tuple-element.19.k1_ref.v1_ref), channel_id=1, source_target_pairs={{0,2},{2,4},{4,6},{6,8},{8,10},{10,12},{12,14},{14,16},{16,18},{18... | collective-permute-start | bytes 3145736 | tf_op jit(solution)/shard_map/ppermute | solution.py:353
  110.7 23.6 %collective-permute-start.4 = (bf16[512,1024]{1,0:T(8,128)(2,1)}, bf16[512,1024]{1,0:T(8,128)(2,1)S(1)}, u32[]{:S(2)}, u32[]{:S(2)}) collective-permute-start(bf16[512,1024]{1,0:T(8,128)(2,1)} %get-tuple-element.18.k0_ref.v0_ref), channel_id=1, source_target_pairs={{0,2},{2,4},{4,6},{6,8},{8,10},{10,12},{12,14},{14,16},{16,18},{18... | collective-permute-start | bytes 3145736 | tf_op jit(solution)/shard_map/ppermute | solution.py:353
  124.3 10.1 %copy-start.6 = (bf16[512,1024]{1,0:T(8,128)(2,1)}, bf16[512,1024]{1,0:T(8,128)(2,1)S(1)}, u32[]{:S(2)}) copy-start(bf16[512,1024]{1,0:T(8,128)(2,1)S(1)} %collective-permute-done.5.k1_ref.v1_ref) | copy-start | bytes 3145732
  134.3 1.0 copy-start.7

commit v3 on v2

v3 whole, which is shorter than its diff:
```python
import functools
import math

import jax
import jax.numpy as jnp
from jax import lax
from jax.experimental import pallas as pl
from jax.experimental.pallas import tpu as pltpu
from jax.sharding import PartitionSpec as P

D = 1024
HEADS = 16
GRID_W = 256
BANDS = 64
TOK = 1024
LOCAL = 512
CAP = 32
MSG = 4 * CAP + 8
BF16 = jnp.bfloat16
F32 = jnp.float32


def iota(shape, dim):
    return lax.broadcasted_iota(jnp.int32, shape, dim)


def ones_where(mask):
    return jnp.where(mask, 1.0, 0.0).astype(BF16)


def params(mebibytes):
    return pltpu.CompilerParams(vmem_limit_bytes=mebibytes * 2**20)


def pack_kernel(cells_ref, feat_ref, out_ref, slot_ref, info_ref):
    step = pl.program_id(0)

    @pl.when(step == 0)
    def _():
        cells = cells_ref[...]
        band = cells >> 10
        within = cells & (TOK - 1)
        member = jnp.where(iota((BANDS, TOK), 0) == band, 1.0, 0.0)
        before = ones_where(iota((TOK, TOK), 0) < iota((TOK, TOK), 1))
        counts = jnp.dot(member.astype(BF16), before, preferred_element_type=F32)
        rank = jnp.sum(member * counts, axis=0, keepdims=True).astype(jnp.int32)
        slot_ref[...] = band * CAP + rank
        place = (within & 768) | ((within & 31) << 3) | ((within >> 5) & 7)
        row = iota((16, TOK), 0)
        info = jnp.where(row == 0, (place >> 5) + 1, jnp.where(row == 1, place & 31, 0))
        info_ref[...] = info.astype(F32).astype(BF16)

    chosen = ones_where(slot_ref[...] - step * PACKED == iota((PACKED, TOK), 0))
    rows = jnp.dot(chosen, feat_ref[...], preferred_element_type=F32).astype(BF16)
    for c in range(4):
        out_ref[:, c * CAP : (c + 1) * CAP, :] = rows[:, c * 128 : (c + 1) * 128].reshape(PACKED // CAP, CAP, 128)
    info = lax.dot_general(
        info_ref[...], chosen, (((1,), (1,)), ((), ())), preferred_element_type=F32
    )
    group = iota((8, 128), 1) // CAP
    for d in range(PACKED // CAP):
        own = jnp.where(group == d % 4, info[:8, d // 4 * 128 : d // 4 * 128 + 128], 0.0)
        own = own + pltpu.roll(own, 64, 1)
        own = own + pltpu.roll(own, 32, 1)
        out_ref[d, 4 * CAP :, :] = own.astype(BF16)


PACKED = 512


def pack(cells, features):
    return pl.pallas_call(
        pack_kernel,
        grid=(BANDS * CAP // PACKED,),
        in_specs=[
            pl.BlockSpec((1, TOK), lambda i: (0, 0)),
            pl.BlockSpec((TOK, LOCAL), lambda i: (0, 0)),
        ],
        out_specs=pl.BlockSpec((PACKED // CAP, MSG, 128), lambda i: (i, 0, 0)),
        out_shape=jax.ShapeDtypeStruct((BANDS, MSG, 128), BF16),
        scratch_shapes=[pltpu.VMEM((1, TOK), jnp.int32), pltpu.VMEM((16, TOK), BF16)],
        compiler_params=params(20),
        name="pack",
    )(cells.reshape(1, TOK), features)


def place_kernel(msg_ref, first_ref, last_ref, place_ref):
    step = pl.program_id(0)

    @pl.when(step == 0)
    def _():
        info = msg_ref[:, 4 * CAP :, :].astype(F32).reshape(16, 4, 8, 128)
        shape = (16, 4, 8, 128)
        info = jnp.sum(jnp.where(iota(shape, 3) // CAP == iota(shape, 1), info, 0.0), axis=1)
        place_ref[...] = (info[:, 0, :] * 32.0 + info[:, 1, :]).astype(jnp.int32) - 32

    cell = iota((256, 128), 0) + step * 256
    chosen = jnp.concatenate(
        [ones_where(place_ref[g : g + 1, :] == cell) for g in range(16)], axis=1
    )
    rows = jnp.concatenate(
        [msg_ref[:, c * CAP : (c + 1) * CAP, :].reshape(BANDS * CAP, 128) for c in range(4)],
        axis=1,
    )
    row = jnp.dot(chosen, rows, preferred_element_type=F32).astype(BF16)

    @pl.when(step < 3)
    def _():
        first_ref[...] = row

    @pl.when(step > 0)
    def _():
        last_ref[...] = row


def place(messages):
    return pl.pallas_call(
        place_kernel,
        grid=(4,),
        in_specs=[pl.BlockSpec((BANDS, MSG, 128), lambda i: (0, 0, 0))],
        out_specs=[
            pl.BlockSpec((256, LOCAL), lambda i: (jnp.minimum(i, 2), 0)),
            pl.BlockSpec((256, LOCAL), lambda i: (jnp.maximum(i - 1, 0), 0)),
        ],
        out_shape=[jax.ShapeDtypeStruct((768, LOCAL), BF16)] * 2,
        scratch_shapes=[pltpu.VMEM((16, 128), jnp.int32)],
        compiler_params=params(20),
        name="place",
    )(messages)


def spread_row(x_ref, r, rows):
    sub = iota((3, 8, 128), 1)
    x = rows.astype(F32).reshape(32, 8, 128)
    x_ref[r, 3:35] = x
    x_ref[r, 0:3] = jnp.where(sub == 0, 0.0, pltpu.roll(x[29:32], 1, 1))
    x_ref[r, 35:38] = jnp.where(sub == 7, 0.0, pltpu.roll(x[0:3], 7, 1))


def spread_taps(tap_ref, w_ref):
    for t in range(49):
        tap_ref[t] = jnp.broadcast_to(w_ref[t : t + 1, :], (8, 128))


def grid_row(ref, at):
    return ref[at * 256 : (at + 1) * 256, :]


def add_taps(acc, x_ref, tap_ref, k, inputs):
    for j in range(7):
        for r, uses in enumerate(inputs):
            taps = [(o, tap_ref[i * 7 + j]) for o, i in uses]
            for n in range(len(acc[0])):
                x = x_ref[r, k + j + n]
                for o, tap in taps:
                    acc[o][n] = acc[o][n] + x * tap


def conv_own_kernel(first_ref, last_ref, w_ref, bias_ref, out_ref, x_ref, tap_ref):
    for r in range(4):
        spread_row(x_ref, r, grid_row(first_ref, r) if r < 3 else grid_row(last_ref, 2))
    spread_taps(tap_ref, w_ref)
    bias = jnp.broadcast_to(bias_ref[...], (8, 128))
    inputs = [[(o, r - o + 3) for o in range(4)] for r in range(4)]

    def group(g, carry):
        k = g * 4
        acc = [[bias] * 4 for _ in range(4)]
        add_taps(acc, x_ref, tap_ref, k, inputs)
        for o in range(4):
            for n in range(4):
                out_ref[o * 32 + k + n] = acc[o][n]
        return carry

    lax.fori_loop(0, 8, group, 0)


def conv_own(first, last, taps, bias):
    column = lambda rows: pl.BlockSpec((rows, 128), lambda i: (0, i))
    return pl.pallas_call(
        conv_own_kernel,
        grid=(4,),
        in_specs=[column(768), column(768), column(49), column(1)],
        out_specs=pl.BlockSpec((128, 8, 128), lambda i: (0, 0, i)),
        out_shape=jax.ShapeDtypeStruct((128, 8, LOCAL), F32),
        scratch_shapes=[pltpu.VMEM((4, 38, 8, 128), F32), pltpu.VMEM((49, 8, 128), F32)],
        compiler_params=params(8),
        cost_estimate=pl.CostEstimate(
            flops=8 * TOK * TOK * LOCAL, bytes_accessed=4 * 2**20, transcendentals=0
        ),
        name="conv_own",
    )(first, last, taps, bias)


def conv_edge_kernel(part_ref, far_ref, near_ref, w_ref, out_ref, x_ref, tap_ref, nat_ref, *, upper):
    sources = [grid_row(far_ref, r) for r in range(3)] + [near_ref[...]]
    for r, rows in enumerate(sources):
        spread_row(x_ref, r, rows)
    spread_taps(tap_ref, w_ref)
    if upper:
        at = [-3, -2, -1, 4]
        outs = [0, 1]
    else:
        at = [4, 5, 6, -1]
        outs = [2, 3]
    inputs = [
        [(o, at[r] - out + 3) for o, out in enumerate(outs) if 0 <= at[r] - out + 3 < 7]
        for r in range(4)
    ]

    def group(g, carry):
        k = g * 8
        acc = [[part_ref[o * 32 + k + n] for n in range(8)] for o in range(2)]
        add_taps(acc, x_ref, tap_ref, k, inputs)
        for o in range(2):
            for n in range(8):
                nat_ref[pl.ds(o * 256 + k + n, 8, stride=32), :] = acc[o][n]
        return carry

    lax.fori_loop(0, 4, group, 0)
    out_ref[...] = nat_ref[...].astype(BF16)


def conv_edge(part, above, below, taps, upper):
    column = lambda rows, at=0: pl.BlockSpec((rows, 128), lambda i: (at, i))
    far, near = (above, below) if upper else (below, above)
    return pl.pallas_call(
        functools.partial(conv_edge_kernel, upper=upper),
        grid=(4,),
        in_specs=[
            pl.BlockSpec((64, 8, 128), lambda i: (0 if upper else 1, 0, i)),
            column(768),
            column(256, 0 if upper else 2),
            column(49),
        ],
        out_specs=column(512),
        out_shape=jax.ShapeDtypeStruct((512, LOCAL), BF16),
        scratch_shapes=[
            pltpu.VMEM((4, 38, 8, 128), F32),
            pltpu.VMEM((49, 8, 128), F32),
            pltpu.VMEM((512, 128), F32),
        ],
        compiler_params=params(8),
        cost_estimate=pl.CostEstimate(
            flops=2 * TOK * TOK * LOCAL, bytes_accessed=4 * 2**20, transcendentals=0
        ),
        name="conv_upper" if upper else "conv_lower",
    )(part, far, near, taps)


def project_kernel(half_ref, own_ref, other_ref, w_own_ref, w_other_ref, kv_ref, q_ref):
    step = pl.program_id(0)
    out = (
        jnp.dot(own_ref[...], w_own_ref[...], preferred_element_type=F32)
        + jnp.dot(other_ref[...], w_other_ref[...], preferred_element_type=F32)
    ).astype(BF16)

    @pl.when(step < 2)
    def _():
        kv_ref[...] = out

    @pl.when(step == 2)
    def _():
        q_ref[...] = out


def project(half, own, other, weights):
    rows = own.shape[0]
    third = lambda j: jnp.where(j == 2, 0, j + 1)
    return pl.pallas_call(
        project_kernel,
        grid_spec=pltpu.PrefetchScalarGridSpec(
            num_scalar_prefetch=1,
            grid=(3,),
            in_specs=[
                pl.BlockSpec((rows, LOCAL), lambda j, h: (0, 0)),
                pl.BlockSpec((rows, LOCAL), lambda j, h: (0, 0)),
                pl.BlockSpec((LOCAL, LOCAL), lambda j, h: (h[0], third(j))),
                pl.BlockSpec((LOCAL, LOCAL), lambda j, h: (1 - h[0], third(j))),
            ],
            out_specs=[
                pl.BlockSpec((rows, LOCAL), lambda j, h: (0, jnp.minimum(j, 1))),
                pl.BlockSpec((rows, LOCAL), lambda j, h: (0, 0)),
            ],
        ),
        out_shape=[
            jax.ShapeDtypeStruct((rows, 2 * LOCAL), BF16),
            jax.ShapeDtypeStruct((rows, LOCAL), BF16),
        ],
        compiler_params=params(12),
        cost_estimate=pl.CostEstimate(
            flops=2 * rows * D * 3 * LOCAL, bytes_accessed=6 * 2**20, transcendentals=0
        ),
        name="project",
    )(half, own, other, weights, weights)


KCHUNK = 256


def partial_attention(queries, keys, values, scores_ref):
    columns = jnp.transpose(values.astype(F32)).astype(BF16)
    ones = jnp.ones((16, keys.shape[0]), BF16)
    columns = [jnp.concatenate([columns[h * 64 : h * 64 + 64], ones], axis=0) for h in range(2)]
    lane = iota(queries[0].shape, 1)
    chunks = [slice(c, c + KCHUNK) for c in range(0, keys.shape[0], KCHUNK)]

    def query(step):
        mine = (lane // 64) == step % 2
        return jnp.where(mine, queries[step // 2] * 0.125, 0.0).astype(BF16)

    def scores(step, at, q, top):
        s = lax.dot_general(keys[at], q, (((1,), (1,)), ((), ())), preferred_element_type=F32)
        scores_ref[step % 2, at, :] = s
        high = jnp.max(s.reshape(KCHUNK // 8, 8, s.shape[1]), axis=0)
        return high if top is None else jnp.maximum(top, high)

    q, top = query(0), None
    for at in chunks:
        top = scores(0, at, q, top)
    steps = 2 * len(queries)
    for step in range(steps):
        top = jnp.max(top, axis=0, keepdims=True)
        q = query(step + 1) if step + 1 < steps else None
        summed = following = None
        for at in chunks:
            if q is not None:
                following = scores(step + 1, at, q, following)
            weight = jnp.exp(scores_ref[step % 2, at, :] - top).astype(BF16)
            part = jnp.dot(columns[step % 2][:, at], weight, preferred_element_type=F32)
            summed = part if summed is None else summed + part
        yield summed[:64], summed[64:65], top
        top = following


def blocks_of(size, *refs):
    return [ref[r : r + size, :] for ref in refs for r in range(0, ref.shape[0], size)]


def stacked(*refs):
    return jnp.concatenate([ref[...] for ref in refs], axis=0)


def attend_kernel(*refs, parts, resumed, final):
    queries, keys, values = refs[:2], refs[2 : 2 + parts], refs[2 + parts : 2 + 2 * parts]
    refs = refs[2 + 2 * parts :]
    if resumed:
        old_acc_ref, old_stat_ref, *refs = refs
    *outs, scores_ref = refs
    size = 512 // parts
    heads = []
    steps = partial_attention(blocks_of(size, *queries), stacked(*keys), stacked(*values), scores_ref)
    for step, (acc, total, top) in enumerate(steps):
        block, head = divmod(step, 2)
        at = slice(block * size, (block + 1) * size)
        rows = slice(head * 64, head * 64 + 64)
        if resumed:
            old_total = old_stat_ref[0, head : head + 1, at]
            old_top = old_stat_ref[0, head + 2 : head + 3, at]
            highest = jnp.maximum(top, old_top)
            here, there = jnp.exp(top - highest), jnp.exp(old_top - highest)
            total = total * here + old_total * there
            acc = acc * here + old_acc_ref[rows, at] * there
            top = highest
        if not final:
            outs[0][rows, at] = acc
            outs[1][0, head : head + 1, at] = total
            outs[1][0, head + 2 : head + 3, at] = top
            continue
        heads.append(acc / total)
        if head:
            outs[0][at, :] = jnp.transpose(jnp.concatenate(heads, axis=0)).astype(BF16)
            heads = []


def attend(queries, keys_values, state=(), final=False):
    column = lambda rows, first=0: pl.BlockSpec((rows, 128), lambda p: (0, first + p))
    parts = len(keys_values)
    count = 512 * parts
    states = [pl.BlockSpec((128, TOK), lambda p: (p, 0)), pl.BlockSpec((1, 8, TOK), lambda p: (p, 0, 0))]
    state_shapes = [
        jax.ShapeDtypeStruct((LOCAL, TOK), F32),
        jax.ShapeDtypeStruct((4, 8, TOK), F32),
    ]
    return pl.pallas_call(
        functools.partial(attend_kernel, parts=parts, resumed=bool(state), final=final),
        grid=(4,),
        in_specs=[column(512)] * (2 + parts) + [column(512, 4)] * parts + (states if state else []),
        out_specs=column(TOK) if final else states,
        out_shape=jax.ShapeDtypeStruct((TOK, LOCAL), BF16) if final else state_shapes,
        scratch_shapes=[pltpu.VMEM((2, count, 512 // parts), F32)],
        compiler_params=params(ATTENTION_VMEM),
        cost_estimate=pl.CostEstimate(
            flops=4 * TOK * count * LOCAL, bytes_accessed=6 * 2**20, transcendentals=8 * TOK * count
        ),
        name="last_keys" if final else ("more_keys" if state else "own_keys"),
    )(*queries, *keys_values, *keys_values, *state)


ATTENTION_VMEM = 24


def merged_taps(conv7, conv5, conv3):
    taps = conv7.astype(F32)
    taps = taps + jnp.pad(conv5.astype(F32), ((1, 1), (1, 1), (0, 0)))
    taps = taps + jnp.pad(conv3.astype(F32), ((2, 2), (2, 2), (0, 0)))
    return taps.reshape(49, LOCAL) + (jnp.arange(49) == 24).astype(F32)[:, None]


def shards(features, cells, conv7, conv5, conv3, conv_bias, w_qkv):
    messages = pack(cells, features)
    arrived = lax.all_to_all(messages, "seq", split_axis=0, concat_axis=0, tiled=True)
    first, last = place(arrived)
    up = [(i, i + 1) for i in range(BANDS - 1)]
    down = [(j, i) for i, j in up]
    above = lax.ppermute(last, "seq", up)
    below = lax.ppermute(first, "seq", down)
    taps = merged_taps(conv7, conv5, conv3)
    bias = conv_bias.astype(F32).reshape(1, LOCAL)
    weights = w_qkv.reshape(D, 3 * LOCAL)
    half = lax.axis_index("head").astype(jnp.int32).reshape(1)
    ring = [(i, (i + 1) % BANDS) for i in range(BANDS)]
    part = conv_own(first, last, taps, bias)
    mixed = [conv_edge(part, above, below, taps, upper) for upper in (False, True)]
    others = [lax.ppermute(own, "head", [(0, 1), (1, 0)]) for own in mixed]
    keys_values, queries = zip(
        *[project(half, own, other, weights) for own, other in zip(mixed, others)]
    )
    first_prior, last_prior = [lax.ppermute(block, "seq", ring) for block in keys_values]
    queries = queries[::-1]
    state = attend(queries, keys_values)
    state = attend(queries, [first_prior], state)
    return attend(queries, [last_prior], state, final=True)


def solution(mesh):
    placed = (
        P("seq", "head"),
        P("seq"),
        P(None, None, "head"),
        P(None, None, "head"),
        P(None, None, "head"),
        P("head"),
        P(None, None, "head"),
    )
    return jax.shard_map(
        shards, mesh=mesh, in_specs=placed, out_specs=P("seq", "head"), check_vma=False
    )
```

time: 150 us -> 133 us (0.89)
  Pallas kernels: 64.4 us -> 55.4 us
  starting transfers between devices: 12.1 us -> 7.82 us
  waiting for transfers between devices: 20.1 us -> 16.2 us
  local copies, waits for them, and re-layouts: 8.08 us -> 9.77 us
    ppermute x2, waiting for transfers between devices: 10 us -> 4.16 us  [shards(): lax.ppermute(block, 'seq', ring)]
    ppermute x1, starting transfers between devices: 8.05 us -> 3.55 us  [shards(): below = lax.ppermute(first, 'seq', down)]
    pallas_call x2, Pallas kernels: 10.9 us -> 7.67 us  [project(): pl.pallas_call(project_kernel, grid_spec=pltpu.PrefetchScalarGridSpec(num...]
    pallas_call x5 -> x7, Pallas kernels: 47.8 us -> 44.7 us  [the longest x3 28.3 us: attend(): pl.pallas_call(functools.partial(attend_kernel, parts=parts, resumed=bool...]
    pallas_call x1, Pallas kernels: 5.6 us -> 3.06 us  [place(): pl.pallas_call(place_kernel, grid=(4,), in_specs=[pl.BlockSpec((BANDS, MS...]
    ppermute x1, waiting for transfers between devices: 6.53 us -> 8.33 us  [shards(): above = lax.ppermute(last, 'seq', up)]
    unnamed x17 -> x13, local copies, waits for them, and re-layouts: 5.1 us -> 6.57 us
  transfers between devices with their start and end apart: 6 -> 6, of which waited for: 5 -> 4; matrix products, arithmetic and copies ran while one was open for 5% -> 6% of each run, Pallas kernels for 21% -> 27%
where the time goes in v3:
time: 133 us; the launch traced here: 132 us
  Pallas kernels  55.4 us (42%)
  blocking collectives  42.7 us (32%)
  waiting for transfers between devices  16.2 us (12%)
  local copies, waits for them, and re-layouts  9.77 us (7%)
  starting transfers between devices  7.82 us (6%)
    all_to_all x1, blocking collectives, shards(): lax.all_to_all(messages, 'seq', split_axis=0, concat_axis=0, tiled=True)  42.7 us
    pallas_call x3, Pallas kernels, attend(): pl.pallas_call(functools.partial(attend_kernel, parts=parts, resumed=bool...  28.3 us
    ppermute x1, waiting for transfers between devices, shards(): above = lax.ppermute(last, 'seq', up)  8.33 us
    pallas_call x2, Pallas kernels, project(): pl.pallas_call(project_kernel, grid_spec=pltpu.PrefetchScalarGridSpec(num...  7.67 us
    unnamed x13, local copies, waits for them, and re-layouts  6.57 us
    pallas_call x2, Pallas kernels, conv_edge(): pl.pallas_call(functools.partial(conv_edge_kernel, upper=upper), grid=(4,...  6.51 us
    pallas_call x1, Pallas kernels, conv_own(): pl.pallas_call(conv_own_kernel, grid=(4,), in_specs=[column(768), column(...  5.22 us
    pallas_call x1, Pallas kernels, pack(): pl.pallas_call(pack_kernel, grid=(BANDS * CAP // PACKED,), in_specs=[pl.B...  4.68 us
  transfers between devices with their start and end apart: 6, of which 4 were waited for; matrix products, arithmetic and copies ran while one was open for 6% of the time, Pallas kernels for 27%

profile of v3, /device:TPU:8, one launch (start us, length us, event | category | flops | bytes accessed | tf_op | source)
XLA Modules:
  0.0 132.2 jit_solution(17853273674540414880)
XLA Ops:
  0.0 1.2 copy-done
  1.2 0.7 copy-done.1
  1.9 4.7 %pack.1 = bf16[64,136,128]{2,1,0:T(8,128)(2,1)S(1)} custom-call(s32[1,1024]{1,0:T(1,128)S(1)} %bitcast.4, bf16[1024,512]{1,0:T(8,128)(2,1)S(1)} %copy-done), custom_call_target="tpu_custom_call" | custom-call | tf_op jit(solution)/shard_map/pack/pallas_call | solution.py:72
  6.6 42.7 %all_to_all.5.msg_ref = bf16[64,136,128]{2,1,0:T(8,128)(2,1)S(1)} all-to-all(bf16[64,136,128]{2,1,0:T(8,128)(2,1)S(1)} %pack.1), channel_id=1, replica_groups=mesh['seq'=64,'head'=2] {'seq'}, dimensions={0} | all-to-all | bytes 4456448 | tf_op jit(solution)/shard_map/all_to_all | solution.py:412
  49.3 3.1 %place.1 = (bf16[768,512]{1,0:T(8,128)(2,1)S(1)}, bf16[768,512]{1,0:T(8,128)(2,1)S(1)}) custom-call(bf16[64,136,128]{2,1,0:T(8,128)(2,1)S(1)} %all_to_all.5.msg_ref), custom_call_target="tpu_custom_call" | custom-call | tf_op jit(solution)/shard_map/place/pallas_call | solution.py:117
  52.4 3.5 %collective-permute-start.1 = (bf16[768,512]{1,0:T(8,128)(2,1)S(1)}, bf16[768,512]{1,0:T(8,128)(2,1)S(1)}, u32[]{:S(2)}, u32[]{:S(2)}) collective-permute-start(bf16[768,512]{1,0:T(8,128)(2,1)S(1)} %get-tuple-element.15.first_ref), channel_id=1, source_target_pairs={{2,0},{4,2},{6,4},{8,6},{10,8},{12,10},{14,12},{16,14},{18,16},{20... | collective-permute-start | bytes 2359304 | tf_op jit(solution)/shard_map/ppermute | solution.py:417
  55.9 1.9 %collective-permute-start = (bf16[768,512]{1,0:T(8,128)(2,1)S(1)}, bf16[768,512]{1,0:T(8,128)(2,1)S(1)}, u32[]{:S(2)}, u32[]{:S(2)}) collective-permute-start(bf16[768,512]{1,0:T(8,128)(2,1)S(1)} %get-tuple-element.16.last_ref), channel_id=1, source_target_pairs={{0,2},{2,4},{4,6},{6,8},{8,10},{10,12},{12,14},{14,16},{16,18},{18... | collective-permute-start | bytes 2359304 | tf_op jit(solution)/shard_map/ppermute | solution.py:416
  57.9 0.0 copy-done.2
  57.9 0.0 copy-done.3
  57.9 0.0 copy-done.4
  57.9 0.0 copy-done.5
  58.0 0.1 broadcast_add_fusion.w_ref
  58.1 5.2 %conv_own.1.part_ref = f32[128,8,512]{2,1,0:T(8,128)S(1)} custom-call(bf16[768,512]{1,0:T(8,128)(2,1)S(1)} %get-tuple-element.15.first_ref, bf16[768,512]{1,0:T(8,128)(2,1)S(1)} %get-tuple-element.16.last_ref, f32[49,512]{1,0:T(8,128)S(1)} %broadcast_add_fusion.w_ref, f32[1,512]{1,0:T(1,128)S(1)} %bitcast.5), custom_call_target="tpu_custom_call" | custom-call | flops 4294967296 | bytes 4194304 | tf_op jit(solution)/shard_map/conv_own/pallas_call | solution.py:180
  63.3 2.1 %collective-permute-done.1.near_ref.far_ref = bf16[768,512]{1,0:T(8,128)(2,1)S(1)} collective-permute-done((bf16[768,512]{1,0:T(8,128)(2,1)S(1)}, bf16[768,512]{1,0:T(8,128)(2,1)S(1)}, u32[]{:S(2)}, u32[]{:S(2)}) %collective-permute-start.1) | collective-permute-done | bytes 786464 | tf_op jit(solution)/shard_map/ppermute | solution.py:417
  65.4 8.3 %collective-permute-done.far_ref.near_ref = bf16[768,512]{1,0:T(8,128)(2,1)S(1)} collective-permute-done((bf16[768,512]{1,0:T(8,128)(2,1)S(1)}, bf16[768,512]{1,0:T(8,128)(2,1)S(1)}, u32[]{:S(2)}, u32[]{:S(2)}) %collective-permute-start) | collective-permute-done | bytes 786464 | tf_op jit(solution)/shard_map/ppermute | solution.py:416
  73.8 3.3 %conv_lower.1.own_ref = bf16[512,512]{1,0:T(8,128)(2,1)} custom-call(f32[128,8,512]{2,1,0:T(8,128)S(1)} %conv_own.1.part_ref, bf16[768,512]{1,0:T(8,128)(2,1)S(1)} %collective-permute-done.1.near_ref.far_ref, bf16[768,512]{1,0:T(8,128)(2,1)S(1)} %collective-permute-done.far_ref.near_ref, f32[49,512]{1,0:T(8,128)S(1)} %broadcast_add_fusion.w_ref), custom_call_target="tpu_custom_call" | custom-call | flops 1073741824 | bytes 4194304 | tf_op jit(solution)/shard_map/conv_lower/pallas_call | solution.py:227
  77.1 0.6 collective-permute-start.3
  77.7 3.2 %conv_upper.1.own_ref = bf16[512,512]{1,0:T(8,128)(2,1)} custom-call(f32[128,8,512]{2,1,0:T(8,128)S(1)} %conv_own.1.part_ref, bf16[768,512]{1,0:T(8,128)(2,1)S(1)} %collective-permute-done.far_ref.near_ref, bf16[768,512]{1,0:T(8,128)(2,1)S(1)} %collective-permute-done.1.near_ref.far_ref, f32[49,512]{1,0:T(8,128)S(1)} %broadcast_add_fusion.w_ref), custom_call_target="tpu_custom_call" | custom-call | flops 1073741824 | bytes 4194304 | tf_op jit(solution)/shard_map/conv_upper/pallas_call | solution.py:227
  80.9 1.4 %collective-permute-start.2 = (bf16[512,512]{1,0:T(8,128)(2,1)}, bf16[512,512]{1,0:T(8,128)(2,1)}, u32[]{:S(2)}, u32[]{:S(2)}) collective-permute-start(bf16[512,512]{1,0:T(8,128)(2,1)} %conv_upper.1.own_ref), channel_id=1, source_target_pairs={{0,1},{1,0},{2,3},{3,2},{4,5},{5,4},{6,7},{7,6},{8,9},{9,8},{10,11... | collective-permute-start | bytes 1572872 | tf_op jit(solution)/shard_map/ppermute | solution.py:425
  82.3 4.6 %copy.9 = bf16[1024,3,512]{0,2,1:T(8,128)(2,1)} copy(bf16[1024,3,512]{2,0,1:T(8,128)(2,1)} %param.13) | data formatting | bytes 6291456 | tf_op args[6]
  86.9 3.2 %copy.10.w_own_ref.w_other_ref = bf16[1024,1536]{1,0:T(8,128)(2,1)S(1)} copy(bf16[1024,1536]{0,1:T(8,128)(2,1)} %bitcast.6) | data formatting | bytes 6291456 | tf_op jit(solution)/shard_map/reshape | solution.py:420
  90.1 0.0 collective-permute-done.3.other_ref
  90.1 3.9 %project.3 = (bf16[512,1024]{1,0:T(8,128)(2,1)S(1)}, bf16[512,512]{1,0:T(8,128)(2,1)S(1)}) custom-call(s32[1]{0:T(128)} %bitcast.half_ref, bf16[512,512]{1,0:T(8,128)(2,1)} %conv_lower.1.own_ref, bf16[512,512]{1,0:T(8,128)(2,1)} %collective-permute-done.3.other_ref, bf16[1024,1536]{1,0:T(8,128)(2,1)S(1)} %copy.10.w_own_ref.w_other_ref, ...), custom_call_target="tpu_custom_call" | custom-call | flops 1610612736 | bytes 6291456 | tf_op jit(solution)/shard_map/project/pallas_call | solution.py:270
  94.0 0.1 collective-permute-start.5
  94.1 1.6 %collective-permute-done.2.other_ref = bf16[512,512]{1,0:T(8,128)(2,1)} collective-permute-done((bf16[512,512]{1,0:T(8,128)(2,1)}, bf16[512,512]{1,0:T(8,128)(2,1)}, u32[]{:S(2)}, u32[]{:S(2)}) %collective-permute-start.2) | collective-permute-done | bytes 524320 | tf_op jit(solution)/shard_map/ppermute | solution.py:425
  95.7 3.8 %project.2 = (bf16[512,1024]{1,0:T(8,128)(2,1)S(1)}, bf16[512,512]{1,0:T(8,128)(2,1)S(1)}) custom-call(s32[1]{0:T(128)} %bitcast.half_ref, bf16[512,512]{1,0:T(8,128)(2,1)} %conv_upper.1.own_ref, bf16[512,512]{1,0:T(8,128)(2,1)} %collective-permute-done.2.other_ref, bf16[1024,1536]{1,0:T(8,128)(2,1)S(1)} %copy.10.w_own_ref.w_other_ref, ...), custom_call_target="tpu_custom_call" | custom-call | flops 1610612736 | bytes 6291456 | tf_op jit(solution)/shard_map/project/pallas_call | solution.py:270
  99.5 0.3 collective-permute-start.4
  99.8 13.1 %own_keys.1 = (f32[512,1024]{1,0:T(8,128)S(1)}, f32[4,8,1024]{2,1,0:T(8,128)S(1)}) custom-call(bf16[512,512]{1,0:T(8,128)(2,1)S(1)} %get-tuple-element.17.refs_0_, bf16[512,512]{1,0:T(8,128)(2,1)S(1)} %get-tuple-element.18.refs_1_, bf16[512,1024]{1,0:T(8,128)(2,1)S(1)} %get-tuple-element.20.refs_2_.refs_4_, ...), custom_call_target="tpu_custom_call" | custom-call | flops 2147483648 | bytes 6291456 | tf_op jit(solution)/shard_map/own_keys/pallas_call | solution.py:385
  112.9 0.0 collective-permute-done.5.refs_2_.refs_3_
  112.9 7.0 %more_keys.1 = (f32[512,1024]{1,0:T(8,128)S(1)}, f32[4,8,1024]{2,1,0:T(8,128)S(1)}) custom-call(bf16[512,512]{1,0:T(8,128)(2,1)S(1)} %get-tuple-element.17.refs_0_, bf16[512,512]{1,0:T(8,128)(2,1)S(1)} %get-tuple-element.18.refs_1_, bf16[512,1024]{1,0:T(8,128)(2,1)S(1)} %collective-permute-done.5.refs_2_.refs_3_, ...), custom_call_target="tpu_custom_call" | custom-call | flops 1073741824 | bytes 6291456 | tf_op jit(solution)/shard_map/more_keys/pallas_call | solution.py:385
  119.9 4.2 %collective-permute-done.4.refs_2_.refs_3_ = bf16[512,1024]{1,0:T(8,128)(2,1)S(1)} collective-permute-done((bf16[512,1024]{1,0:T(8,128)(2,1)S(1)}, bf16[512,1024]{1,0:T(8,128)(2,1)S(1)}, u32[]{:S(2)}, u32[]{:S(2)}) %collective-permute-start.4) | collective-permute-done | bytes 1048608 | tf_op jit(solution)/shard_map/ppermute | solution.py:429
  124.0 8.2 %last_keys.1 = bf16[1024,512]{1,0:T(8,128)(2,1)} custom-call(bf16[512,512]{1,0:T(8,128)(2,1)S(1)} %get-tuple-element.17.refs_0_, bf16[512,512]{1,0:T(8,128)(2,1)S(1)} %get-tuple-element.18.refs_1_, bf16[512,1024]{1,0:T(8,128)(2,1)S(1)} %collective-permute-done.4.refs_2_.refs_3_, bf16[512,1024]{1,0:T(8,128)(2,1)S(1)} %collective-permute-done.4.refs_2_.refs_3_, ...), custom_call_target="tpu_custom_call" | custom-call | flops 1073741824 | bytes 6291456 | tf_op jit(solution)/shard_map/last_keys/pallas_call | solution.py:385
  (10 shorter events, 0.1 us)
Async XLA Ops:
  0.0 1.2 copy-start
  1.2 0.7 copy-start.1
  49.3 8.6 %copy-start.2 = (bf16[7,7,512]{2,1,0:T(8,128)(2,1)S(1)}, bf16[7,7,512]{2,1,0:T(8,128)(2,1)}, u32[]{:S(2)}) copy-start(bf16[7,7,512]{2,1,0:T(8,128)(2,1)} %param.9) | copy-start | bytes 150532
  49.3 8.6 %copy-start.3 = (bf16[5,5,512]{2,1,0:T(8,128)(2,1)S(1)}, bf16[5,5,512]{2,1,0:T(8,128)(2,1)}, u32[]{:S(2)}) copy-start(bf16[5,5,512]{2,1,0:T(8,128)(2,1)} %param.10) | copy-start | bytes 76804
  49.3 8.6 %copy-start.4 = (bf16[3,3,512]{2,1,0:T(4,128)(2,1)S(1)}, bf16[3,3,512]{2,1,0:T(4,128)(2,1)}, u32[]{:S(2)}) copy-start(bf16[3,3,512]{2,1,0:T(4,128)(2,1)} %param.11) | copy-start | bytes 27652
  49.3 8.6 %copy-start.5 = (bf16[512]{0:T(512)(128)(2,1)S(1)}, bf16[512]{0:T(512)(128)(2,1)}, u32[]{:S(2)}) copy-start(bf16[512]{0:T(512)(128)(2,1)} %param.12) | copy-start | bytes 3076
  52.4 13.0 %collective-permute-start.1 = (bf16[768,512]{1,0:T(8,128)(2,1)S(1)}, bf16[768,512]{1,0:T(8,128)(2,1)S(1)}, u32[]{:S(2)}, u32[]{:S(2)}) collective-permute-start(bf16[768,512]{1,0:T(8,128)(2,1)S(1)} %get-tuple-element.15.first_ref), channel_id=1, source_target_pairs={{2,0},{4,2},{6,4},{8,6},{10,8},{12,10},{14,12},{16,14},{18,16},{20... | collective-permute-start | bytes 2359304 | tf_op jit(solution)/shard_map/ppermute | solution.py:417
  55.9 17.8 %collective-permute-start = (bf16[768,512]{1,0:T(8,128)(2,1)S(1)}, bf16[768,512]{1,0:T(8,128)(2,1)S(1)}, u32[]{:S(2)}, u32[]{:S(2)}) collective-permute-start(bf16[768,512]{1,0:T(8,128)(2,1)S(1)} %get-tuple-element.16.last_ref), channel_id=1, source_target_pairs={{0,2},{2,4},{4,6},{6,8},{8,10},{10,12},{12,14},{14,16},{16,18},{18... | collective-permute-start | bytes 2359304 | tf_op jit(solution)/shard_map/ppermute | solution.py:416
  77.1 13.1 %collective-permute-start.3 = (bf16[512,512]{1,0:T(8,128)(2,1)}, bf16[512,512]{1,0:T(8,128)(2,1)}, u32[]{:S(2)}, u32[]{:S(2)}) collective-permute-start(bf16[512,512]{1,0:T(8,128)(2,1)} %conv_lower.1.own_ref), channel_id=1, source_target_pairs={{0,1},{1,0},{2,3},{3,2},{4,5},{5,4},{6,7},{7,6},{8,9},{9,8},{10,11... | collective-permute-start | bytes 1572872 | tf_op jit(solution)/shard_map/ppermute | solution.py:425
  80.9 14.8 %collective-permute-start.2 = (bf16[512,512]{1,0:T(8,128)(2,1)}, bf16[512,512]{1,0:T(8,128)(2,1)}, u32[]{:S(2)}, u32[]{:S(2)}) collective-permute-start(bf16[512,512]{1,0:T(8,128)(2,1)} %conv_upper.1.own_ref), channel_id=1, source_target_pairs={{0,1},{1,0},{2,3},{3,2},{4,5},{5,4},{6,7},{7,6},{8,9},{9,8},{10,11... | collective-permute-start | bytes 1572872 | tf_op jit(solution)/shard_map/ppermute | solution.py:425
  94.0 18.9 %collective-permute-start.5 = (bf16[512,1024]{1,0:T(8,128)(2,1)S(1)}, bf16[512,1024]{1,0:T(8,128)(2,1)S(1)}, u32[]{:S(2)}, u32[]{:S(2)}) collective-permute-start(bf16[512,1024]{1,0:T(8,128)(2,1)S(1)} %get-tuple-element.20.refs_2_.refs_4_), channel_id=1, source_target_pairs={{0,2},{2,4},{4,6},{6,8},{8,10},{10,12},{12,14},{14,16},{16,18},{18... | collective-permute-start | bytes 3145736 | tf_op jit(solution)/shard_map/ppermute | solution.py:429
  99.5 24.5 %collective-permute-start.4 = (bf16[512,1024]{1,0:T(8,128)(2,1)S(1)}, bf16[512,1024]{1,0:T(8,128)(2,1)S(1)}, u32[]{:S(2)}, u32[]{:S(2)}) collective-permute-start(bf16[512,1024]{1,0:T(8,128)(2,1)S(1)} %get-tuple-element.19.refs_3_.refs_5_), channel_id=1, source_target_pairs={{0,2},{2,4},{4,6},{6,8},{8,10},{10,12},{12,14},{14,16},{16,18},{18... | collective-permute-start | bytes 3145736 | tf_op jit(solution)/shard_map/ppermute | solution.py:429

commit v4 on v3

--- a/solution.py
+++ b/solution.py
@@ -218,7 +218,7 @@
         return carry
 
     lax.fori_loop(0, 4, group, 0)
-    out_ref[...] = nat_ref[...].astype(BF16)
+    out_ref[...] = nat_ref[:512, :].astype(BF16)
 
 
 def conv_edge(part, above, below, taps, upper):
@@ -238,7 +238,7 @@
         scratch_shapes=[
             pltpu.VMEM((4, 38, 8, 128), F32),
             pltpu.VMEM((49, 8, 128), F32),
-            pltpu.VMEM((512, 128), F32),
+            pltpu.VMEM((512 + 32, 128), F32),
         ],
         compiler_params=params(8),
         cost_estimate=pl.CostEstimate(
@@ -248,51 +248,60 @@
     )(part, far, near, taps)
 
 
-def project_kernel(half_ref, own_ref, other_ref, w_own_ref, w_other_ref, kv_ref, q_ref):
-    step = pl.program_id(0)
-    out = (
-        jnp.dot(own_ref[...], w_own_ref[...], preferred_element_type=F32)
-        + jnp.dot(other_ref[...], w_other_ref[...], preferred_element_type=F32)
-    ).astype(BF16)
-
-    @pl.when(step < 2)
-    def _():
-        kv_ref[...] = out
-
-    @pl.when(step == 2)
-    def _():
-        q_ref[...] = out
+def project_kernel(half_ref, own_ref, other_ref, w_ref, kv_ref, q_ref, held_ref, sems):
+    mine = pl.multiple_of(half_ref[0] * LOCAL, LOCAL)
+    theirs = pl.multiple_of((1 - half_ref[0]) * LOCAL, LOCAL)
+    copies = []
+    for step, third in enumerate((1, 2, 0)):
+        for side, start in enumerate((mine, theirs)):
+            copies.append(
+                pltpu.make_async_copy(
+                    w_ref.at[third, pl.ds(start, LOCAL), :], held_ref.at[step, side], sems.at[step, side]
+                )
+            )
+            copies[-1].start()
+    own, other = own_ref[...], other_ref[...]
+    for step in range(3):
+        copies[2 * step].wait()
+        copies[2 * step + 1].wait()
+        out = (
+            jnp.dot(own, held_ref[step, 0], preferred_element_type=F32)
+            + jnp.dot(other, held_ref[step, 1], preferred_element_type=F32)
+        ).astype(BF16)
+        if step < 2:
+            kv_ref[:, step * LOCAL : (step + 1) * LOCAL] = out
+        else:
+            q_ref[...] = out
 
 
 def project(half, own, other, weights):
     rows = own.shape[0]
-    third = lambda j: jnp.where(j == 2, 0, j + 1)
     return pl.pallas_call(
         project_kernel,
-        grid_spec=pltpu.PrefetchScalarGridSpec(
-            num_scalar_prefetch=1,
-            grid=(3,),
-            in_specs=[
-                pl.BlockSpec((rows, LOCAL), lambda j, h: (0, 0)),
-                pl.BlockSpec((rows, LOCAL), lambda j, h: (0, 0)),
-                pl.BlockSpec((LOCAL, LOCAL), lambda j, h: (h[0], third(j))),
-                pl.BlockSpec((LOCAL, LOCAL), lambda j, h: (1 - h[0], third(j))),
-            ],
-            out_specs=[
-                pl.BlockSpec((rows, LOCAL), lambda j, h: (0, jnp.minimum(j, 1))),
-                pl.BlockSpec((rows, LOCAL), lambda j, h: (0, 0)),
-            ],
-        ),
+        in_specs=[
+            pl.BlockSpec(memory_space=pltpu.SMEM),
+            pl.BlockSpec((rows, LOCAL), lambda: (0, 0)),
+            pl.BlockSpec((rows, LOCAL), lambda: (0, 0)),
+            pl.BlockSpec(memory_space=pltpu.HBM),
+        ],
+        out_specs=[
+            pl.BlockSpec((rows, 2 * LOCAL), lambda: (0, 0)),
+            pl.BlockSpec((rows, LOCAL), lambda: (0, 0)),
+        ],
         out_shape=[
             jax.ShapeDtypeStruct((rows, 2 * LOCAL), BF16),
             jax.ShapeDtypeStruct((rows, LOCAL), BF16),
         ],
-        compiler_params=params(12),
+        scratch_shapes=[
+            pltpu.VMEM((3, 2, LOCAL, LOCAL), BF16),
+            pltpu.SemaphoreType.DMA((3, 2)),
+        ],
+        compiler_params=params(16),
         cost_estimate=pl.CostEstimate(
             flops=2 * rows * D * 3 * LOCAL, bytes_accessed=6 * 2**20, transcendentals=0
         ),
         name="project",
-    )(half, own, other, weights, weights)
+    )(half, own, other, weights)
 
 
 KCHUNK = 256
@@ -417,7 +426,7 @@
     below = lax.ppermute(first, "seq", down)
     taps = merged_taps(conv7, conv5, conv3)
     bias = conv_bias.astype(F32).reshape(1, LOCAL)
-    weights = w_qkv.reshape(D, 3 * LOCAL)
+    weights = jnp.transpose(w_qkv, (1, 0, 2))
     half = lax.axis_index("head").astype(jnp.int32).reshape(1)
     ring = [(i, (i + 1) % BANDS) for i in range(BANDS)]
     part = conv_own(first, last, taps, bias)

time: 133 us -> 132 us (level)
  waiting for transfers between devices: 16.2 us -> 25.5 us
  local copies, waits for them, and re-layouts: 9.77 us -> 3.84 us
  Pallas kernels: 55.4 us -> 51.5 us
    ppermute x2, waiting for transfers between devices: 1.61 us -> 9.11 us  [shards(): others = [lax.ppermute(own, 'head', [(0, 1), (1, 0)]) for own in mixed]]
    reshape x1 -> x0, local copies, waits for them, and re-layouts: 3.18 us -> none  [shards(): weights = w_qkv.reshape(D, 3 * LOCAL)]
    pallas_call x2, Pallas kernels: 7.67 us -> 4.91 us  [project(): pl.pallas_call(project_kernel, in_specs=[pl.BlockSpec(memory_space=pltpu....]
    unnamed x13 -> x16, local copies, waits for them, and re-layouts: 6.57 us -> 3.82 us
    ppermute x2, waiting for transfers between devices: 4.16 us -> 5.97 us  [shards(): lax.ppermute(block, 'seq', ring)]
  transfers between devices with their start and end apart: 6 -> 6, of which waited for: 4 -> 6; matrix products, arithmetic and copies ran while one was open for 6% -> 0% of each run, Pallas kernels for 27% -> 25%
where the time goes in v4:
time: 132 us
  Pallas kernels  51.5 us (39%)
  blocking collectives  42.7 us (32%)
  waiting for transfers between devices  25.5 us (19%)
  starting transfers between devices  7.98 us (6%)
  local copies, waits for them, and re-layouts  3.84 us (3%)
    all_to_all x1, blocking collectives, shards(): lax.all_to_all(messages, 'seq', split_axis=0, concat_axis=0, tiled=True)  42.7 us
    pallas_call x3, Pallas kernels, attend(): pl.pallas_call(functools.partial(attend_kernel, parts=parts, resumed=bool...  28.2 us
    ppermute x2, waiting for transfers between devices, shards(): others = [lax.ppermute(own, 'head', [(0, 1), (1, 0)]) for own in mixed]  9.11 us
    ppermute x1, waiting for transfers between devices, shards(): above = lax.ppermute(last, 'seq', up)  8.33 us
    ppermute x2, waiting for transfers between devices, shards(): lax.ppermute(block, 'seq', ring)  5.97 us
    pallas_call x2, Pallas kernels, conv_edge(): pl.pallas_call(functools.partial(conv_edge_kernel, upper=upper), grid=(4,...  5.34 us
    pallas_call x1, Pallas kernels, conv_own(): pl.pallas_call(conv_own_kernel, grid=(4,), in_specs=[column(768), column(...  5.22 us
    pallas_call x2, Pallas kernels, project(): pl.pallas_call(project_kernel, in_specs=[pl.BlockSpec(memory_space=pltpu....  4.91 us
  transfers between devices with their start and end apart: 6, of which 6 were waited for; matrix products, arithmetic and copies ran while one was open for 0% of the time, Pallas kernels for 25%

profile of v4, /device:TPU:8, one launch (start us, length us, event | category | flops | bytes accessed | tf_op | source)
XLA Modules:
  0.0 131.8 jit_solution(8753041897287190874)
XLA Ops:
  0.0 1.2 copy-done
  1.2 0.7 copy-done.1
  1.9 4.7 %pack.1 = bf16[64,136,128]{2,1,0:T(8,128)(2,1)S(1)} custom-call(s32[1,1024]{1,0:T(1,128)S(1)} %bitcast.4, bf16[1024,512]{1,0:T(8,128)(2,1)S(1)} %copy-done), custom_call_target="tpu_custom_call" | custom-call | tf_op jit(solution)/shard_map/pack/pallas_call | solution.py:72
  6.6 42.7 %all_to_all.5.msg_ref = bf16[64,136,128]{2,1,0:T(8,128)(2,1)S(1)} all-to-all(bf16[64,136,128]{2,1,0:T(8,128)(2,1)S(1)} %pack.1), channel_id=1, replica_groups=mesh['seq'=64,'head'=2] {'seq'}, dimensions={0} | all-to-all | bytes 4456448 | tf_op jit(solution)/shard_map/all_to_all | solution.py:421
  49.3 3.1 %place.1 = (bf16[768,512]{1,0:T(8,128)(2,1)S(1)}, bf16[768,512]{1,0:T(8,128)(2,1)S(1)}) custom-call(bf16[64,136,128]{2,1,0:T(8,128)(2,1)S(1)} %all_to_all.5.msg_ref), custom_call_target="tpu_custom_call" | custom-call | tf_op jit(solution)/shard_map/place/pallas_call | solution.py:117
  52.4 3.5 %collective-permute-start.1 = (bf16[768,512]{1,0:T(8,128)(2,1)S(1)}, bf16[768,512]{1,0:T(8,128)(2,1)S(1)}, u32[]{:S(2)}, u32[]{:S(2)}) collective-permute-start(bf16[768,512]{1,0:T(8,128)(2,1)S(1)} %get-tuple-element.15.first_ref), channel_id=1, source_target_pairs={{2,0},{4,2},{6,4},{8,6},{10,8},{12,10},{14,12},{16,14},{18,16},{20... | collective-permute-start | bytes 2359304 | tf_op jit(solution)/shard_map/ppermute | solution.py:426
  55.9 1.9 %collective-permute-start = (bf16[768,512]{1,0:T(8,128)(2,1)S(1)}, bf16[768,512]{1,0:T(8,128)(2,1)S(1)}, u32[]{:S(2)}, u32[]{:S(2)}) collective-permute-start(bf16[768,512]{1,0:T(8,128)(2,1)S(1)} %get-tuple-element.16.last_ref), channel_id=1, source_target_pairs={{0,2},{2,4},{4,6},{6,8},{8,10},{10,12},{12,14},{14,16},{16,18},{18... | collective-permute-start | bytes 2359304 | tf_op jit(solution)/shard_map/ppermute | solution.py:425
  57.9 0.0 copy-done.4
  57.9 0.0 copy-done.5
  57.9 0.0 copy-done.6
  57.9 0.0 copy-done.7
  58.0 0.1 broadcast_add_fusion.w_ref
  58.1 5.2 %conv_own.1.part_ref = f32[128,8,512]{2,1,0:T(8,128)S(1)} custom-call(bf16[768,512]{1,0:T(8,128)(2,1)S(1)} %get-tuple-element.15.first_ref, bf16[768,512]{1,0:T(8,128)(2,1)S(1)} %get-tuple-element.16.last_ref, f32[49,512]{1,0:T(8,128)S(1)} %broadcast_add_fusion.w_ref, f32[1,512]{1,0:T(1,128)S(1)} %bitcast.5), custom_call_target="tpu_custom_call" | custom-call | flops 4294967296 | bytes 4194304 | tf_op jit(solution)/shard_map/conv_own/pallas_call | solution.py:180
  63.3 2.1 %collective-permute-done.1.near_ref.far_ref = bf16[768,512]{1,0:T(8,128)(2,1)S(1)} collective-permute-done((bf16[768,512]{1,0:T(8,128)(2,1)S(1)}, bf16[768,512]{1,0:T(8,128)(2,1)S(1)}, u32[]{:S(2)}, u32[]{:S(2)}) %collective-permute-start.1) | collective-permute-done | bytes 786464 | tf_op jit(solution)/shard_map/ppermute | solution.py:426
  65.4 8.3 %collective-permute-done.far_ref.near_ref = bf16[768,512]{1,0:T(8,128)(2,1)S(1)} collective-permute-done((bf16[768,512]{1,0:T(8,128)(2,1)S(1)}, bf16[768,512]{1,0:T(8,128)(2,1)S(1)}, u32[]{:S(2)}, u32[]{:S(2)}) %collective-permute-start) | collective-permute-done | bytes 786464 | tf_op jit(solution)/shard_map/ppermute | solution.py:425
  73.8 2.7 %conv_lower.1.own_ref = bf16[512,512]{1,0:T(8,128)(2,1)S(1)} custom-call(f32[128,8,512]{2,1,0:T(8,128)S(1)} %conv_own.1.part_ref, bf16[768,512]{1,0:T(8,128)(2,1)S(1)} %collective-permute-done.1.near_ref.far_ref, bf16[768,512]{1,0:T(8,128)(2,1)S(1)} %collective-permute-done.far_ref.near_ref, f32[49,512]{1,0:T(8,128)S(1)} %broadcast_add_fusion.w_ref), custom_call_target="tpu_custom_call" | custom-call | flops 1073741824 | bytes 4194304 | tf_op jit(solution)/shard_map/conv_lower/pallas_call | solution.py:227
  76.5 0.7 collective-permute-start.3
  77.2 2.6 %conv_upper.1.own_ref = bf16[512,512]{1,0:T(8,128)(2,1)S(1)} custom-call(f32[128,8,512]{2,1,0:T(8,128)S(1)} %conv_own.1.part_ref, bf16[768,512]{1,0:T(8,128)(2,1)S(1)} %collective-permute-done.far_ref.near_ref, bf16[768,512]{1,0:T(8,128)(2,1)S(1)} %collective-permute-done.1.near_ref.far_ref, f32[49,512]{1,0:T(8,128)S(1)} %broadcast_add_fusion.w_ref), custom_call_target="tpu_custom_call" | custom-call | flops 1073741824 | bytes 4194304 | tf_op jit(solution)/shard_map/conv_upper/pallas_call | solution.py:227
  79.8 1.5 %collective-permute-start.2 = (bf16[512,512]{1,0:T(8,128)(2,1)S(1)}, bf16[512,512]{1,0:T(8,128)(2,1)S(1)}, u32[]{:S(2)}, u32[]{:S(2)}) collective-permute-start(bf16[512,512]{1,0:T(8,128)(2,1)S(1)} %conv_upper.1.own_ref), channel_id=1, source_target_pairs={{0,1},{1,0},{2,3},{3,2},{4,5},{5,4},{6,7},{7,6},{8,9},{9,8},{10,11... | collective-permute-start | bytes 1572872 | tf_op jit(solution)/shard_map/ppermute | solution.py:434
  81.3 7.9 %collective-permute-done.3.other_ref = bf16[512,512]{1,0:T(8,128)(2,1)S(1)} collective-permute-done((bf16[512,512]{1,0:T(8,128)(2,1)S(1)}, bf16[512,512]{1,0:T(8,128)(2,1)S(1)}, u32[]{:S(2)}, u32[]{:S(2)}) %collective-permute-start.3) | collective-permute-done | bytes 524320 | tf_op jit(solution)/shard_map/ppermute | solution.py:434
  89.2 1.9 %copy-done.2 = bf16[1024,3,512]{2,0,1:T(8,128)(2,1)S(1)} copy-done((bf16[1024,3,512]{2,0,1:T(8,128)(2,1)S(1)}, bf16[1024,3,512]{2,0,1:T(8,128)(2,1)}, u32[]{:S(2)}) %copy-start.2) | copy-done | bytes 3145752
  91.1 2.5 %project.3 = (bf16[512,1024]{1,0:T(8,128)(2,1)S(1)}, bf16[512,512]{1,0:T(8,128)(2,1)S(1)}) custom-call(s32[1]{0:T(128)} %bitcast.half_ref, bf16[512,512]{1,0:T(8,128)(2,1)S(1)} %conv_lower.1.own_ref, bf16[512,512]{1,0:T(8,128)(2,1)S(1)} %collective-permute-done.3.other_ref, bf16[3,1024,512]{2,1,0:T(8,128)(2,1)S(1)} %bitcast.6), custom_call_target="tpu_custom_call" | custom-call | flops 1610612736 | bytes 6291456 | tf_op jit(solution)/shard_map/project/pallas_call | solution.py:279
  93.6 0.1 collective-permute-start.5
  93.7 1.2 collective-permute-done.2.other_ref
  94.8 0.0 copy-done.3
  94.9 2.5 %project.2 = (bf16[512,1024]{1,0:T(8,128)(2,1)S(1)}, bf16[512,512]{1,0:T(8,128)(2,1)S(1)}) custom-call(s32[1]{0:T(128)} %bitcast.half_ref, bf16[512,512]{1,0:T(8,128)(2,1)S(1)} %conv_upper.1.own_ref, bf16[512,512]{1,0:T(8,128)(2,1)S(1)} %collective-permute-done.2.other_ref, bf16[3,1024,512]{2,1,0:T(8,128)(2,1)S(1)} %bitcast.7), custom_call_target="tpu_custom_call" | custom-call | flops 1610612736 | bytes 6291456 | tf_op jit(solution)/shard_map/project/pallas_call | solution.py:279
  97.3 0.3 collective-permute-start.4
  97.6 13.1 %own_keys.1 = (f32[512,1024]{1,0:T(8,128)S(1)}, f32[4,8,1024]{2,1,0:T(8,128)S(1)}) custom-call(bf16[512,512]{1,0:T(8,128)(2,1)S(1)} %get-tuple-element.17.refs_0_, bf16[512,512]{1,0:T(8,128)(2,1)S(1)} %get-tuple-element.18.refs_1_, bf16[512,1024]{1,0:T(8,128)(2,1)S(1)} %get-tuple-element.20.refs_2_.refs_4_, ...), custom_call_target="tpu_custom_call" | custom-call | flops 2147483648 | bytes 6291456 | tf_op jit(solution)/shard_map/own_keys/pallas_call | solution.py:394
  110.7 1.7 %collective-permute-done.5.refs_2_.refs_3_ = bf16[512,1024]{1,0:T(8,128)(2,1)S(1)} collective-permute-done((bf16[512,1024]{1,0:T(8,128)(2,1)S(1)}, bf16[512,1024]{1,0:T(8,128)(2,1)S(1)}, u32[]{:S(2)}, u32[]{:S(2)}) %collective-permute-start.5) | collective-permute-done | bytes 1048608 | tf_op jit(solution)/shard_map/ppermute | solution.py:438
  112.4 7.0 %more_keys.1 = (f32[512,1024]{1,0:T(8,128)S(1)}, f32[4,8,1024]{2,1,0:T(8,128)S(1)}) custom-call(bf16[512,512]{1,0:T(8,128)(2,1)S(1)} %get-tuple-element.17.refs_0_, bf16[512,512]{1,0:T(8,128)(2,1)S(1)} %get-tuple-element.18.refs_1_, bf16[512,1024]{1,0:T(8,128)(2,1)S(1)} %collective-permute-done.5.refs_2_.refs_3_, ...), custom_call_target="tpu_custom_call" | custom-call | flops 1073741824 | bytes 6291456 | tf_op jit(solution)/shard_map/more_keys/pallas_call | solution.py:394
  119.4 4.2 %collective-permute-done.4.refs_2_.refs_3_ = bf16[512,1024]{1,0:T(8,128)(2,1)S(1)} collective-permute-done((bf16[512,1024]{1,0:T(8,128)(2,1)S(1)}, bf16[512,1024]{1,0:T(8,128)(2,1)S(1)}, u32[]{:S(2)}, u32[]{:S(2)}) %collective-permute-start.4) | collective-permute-done | bytes 1048608 | tf_op jit(solution)/shard_map/ppermute | solution.py:438
  123.6 8.2 %last_keys.1 = bf16[1024,512]{1,0:T(8,128)(2,1)} custom-call(bf16[512,512]{1,0:T(8,128)(2,1)S(1)} %get-tuple-element.17.refs_0_, bf16[512,512]{1,0:T(8,128)(2,1)S(1)} %get-tuple-element.18.refs_1_, bf16[512,1024]{1,0:T(8,128)(2,1)S(1)} %collective-permute-done.4.refs_2_.refs_3_, bf16[512,1024]{1,0:T(8,128)(2,1)S(1)} %collective-permute-done.4.refs_2_.refs_3_, ...), custom_call_target="tpu_custom_call" | custom-call | flops 1073741824 | bytes 6291456 | tf_op jit(solution)/shard_map/last_keys/pallas_call | solution.py:394
  (12 shorter events, 0.1 us)
Async XLA Ops:
  0.0 1.2 copy-start
  1.2 0.7 copy-start.1
  49.3 8.6 %copy-start.4 = (bf16[7,7,512]{2,1,0:T(8,128)(2,1)S(1)}, bf16[7,7,512]{2,1,0:T(8,128)(2,1)}, u32[]{:S(2)}) copy-start(bf16[7,7,512]{2,1,0:T(8,128)(2,1)} %param.9) | copy-start | bytes 150532
  49.3 8.6 %copy-start.5 = (bf16[5,5,512]{2,1,0:T(8,128)(2,1)S(1)}, bf16[5,5,512]{2,1,0:T(8,128)(2,1)}, u32[]{:S(2)}) copy-start(bf16[5,5,512]{2,1,0:T(8,128)(2,1)} %param.10) | copy-start | bytes 76804
  49.3 8.6 %copy-start.6 = (bf16[3,3,512]{2,1,0:T(4,128)(2,1)S(1)}, bf16[3,3,512]{2,1,0:T(4,128)(2,1)}, u32[]{:S(2)}) copy-start(bf16[3,3,512]{2,1,0:T(4,128)(2,1)} %param.11) | copy-start | bytes 27652
  49.3 8.6 %copy-start.7 = (bf16[512]{0:T(512)(128)(2,1)S(1)}, bf16[512]{0:T(512)(128)(2,1)}, u32[]{:S(2)}) copy-start(bf16[512]{0:T(512)(128)(2,1)} %param.12) | copy-start | bytes 3076
  52.4 13.0 %collective-permute-start.1 = (bf16[768,512]{1,0:T(8,128)(2,1)S(1)}, bf16[768,512]{1,0:T(8,128)(2,1)S(1)}, u32[]{:S(2)}, u32[]{:S(2)}) collective-permute-start(bf16[768,512]{1,0:T(8,128)(2,1)S(1)} %get-tuple-element.15.first_ref), channel_id=1, source_target_pairs={{2,0},{4,2},{6,4},{8,6},{10,8},{12,10},{14,12},{16,14},{18,16},{20... | collective-permute-start | bytes 2359304 | tf_op jit(solution)/shard_map/ppermute | solution.py:426
  55.9 17.8 %collective-permute-start = (bf16[768,512]{1,0:T(8,128)(2,1)S(1)}, bf16[768,512]{1,0:T(8,128)(2,1)S(1)}, u32[]{:S(2)}, u32[]{:S(2)}) collective-permute-start(bf16[768,512]{1,0:T(8,128)(2,1)S(1)} %get-tuple-element.16.last_ref), channel_id=1, source_target_pairs={{0,2},{2,4},{4,6},{6,8},{8,10},{10,12},{12,14},{14,16},{16,18},{18... | collective-permute-start | bytes 2359304 | tf_op jit(solution)/shard_map/ppermute | solution.py:425
  76.5 12.8 %collective-permute-start.3 = (bf16[512,512]{1,0:T(8,128)(2,1)S(1)}, bf16[512,512]{1,0:T(8,128)(2,1)S(1)}, u32[]{:S(2)}, u32[]{:S(2)}) collective-permute-start(bf16[512,512]{1,0:T(8,128)(2,1)S(1)} %conv_lower.1.own_ref), channel_id=1, source_target_pairs={{0,1},{1,0},{2,3},{3,2},{4,5},{5,4},{6,7},{7,6},{8,9},{9,8},{10,11... | collective-permute-start | bytes 1572872 | tf_op jit(solution)/shard_map/ppermute | solution.py:434
  79.8 15.1 %collective-permute-start.2 = (bf16[512,512]{1,0:T(8,128)(2,1)S(1)}, bf16[512,512]{1,0:T(8,128)(2,1)S(1)}, u32[]{:S(2)}, u32[]{:S(2)}) collective-permute-start(bf16[512,512]{1,0:T(8,128)(2,1)S(1)} %conv_upper.1.own_ref), channel_id=1, source_target_pairs={{0,1},{1,0},{2,3},{3,2},{4,5},{5,4},{6,7},{7,6},{8,9},{9,8},{10,11... | collective-permute-start | bytes 1572872 | tf_op jit(solution)/shard_map/ppermute | solution.py:434
  89.2 1.9 %copy-start.2 = (bf16[1024,3,512]{2,0,1:T(8,128)(2,1)S(1)}, bf16[1024,3,512]{2,0,1:T(8,128)(2,1)}, u32[]{:S(2)}) copy-start(bf16[1024,3,512]{2,0,1:T(8,128)(2,1)} %param.13) | copy-start | bytes 9437188
  91.1 3.7 %copy-start.3 = (bf16[1024,3,512]{2,0,1:T(8,128)(2,1)S(1)}, bf16[1024,3,512]{2,0,1:T(8,128)(2,1)}, u32[]{:S(2)}) copy-start(bf16[1024,3,512]{2,0,1:T(8,128)(2,1)} %param.13) | copy-start | bytes 9437188
  93.6 18.8 %collective-permute-start.5 = (bf16[512,1024]{1,0:T(8,128)(2,1)S(1)}, bf16[512,1024]{1,0:T(8,128)(2,1)S(1)}, u32[]{:S(2)}, u32[]{:S(2)}) collective-permute-start(bf16[512,1024]{1,0:T(8,128)(2,1)S(1)} %get-tuple-element.20.refs_2_.refs_4_), channel_id=1, source_target_pairs={{0,2},{2,4},{4,6},{6,8},{8,10},{10,12},{12,14},{14,16},{16,18},{18... | collective-permute-start | bytes 3145736 | tf_op jit(solution)/shard_map/ppermute | solution.py:438
  97.3 26.3 %collective-permute-start.4 = (bf16[512,1024]{1,0:T(8,128)(2,1)S(1)}, bf16[512,1024]{1,0:T(8,128)(2,1)S(1)}, u32[]{:S(2)}, u32[]{:S(2)}) collective-permute-start(bf16[512,1024]{1,0:T(8,128)(2,1)S(1)} %get-tuple-element.19.refs_3_.refs_5_), channel_id=1, source_target_pairs={{0,2},{2,4},{4,6},{6,8},{8,10},{10,12},{12,14},{14,16},{16,18},{18... | collective-permute-start | bytes 3145736 | tf_op jit(solution)/shard_map/ppermute | solution.py:438
